TPU v7x, 512 devices: a whole 4x4x16 slice. The times are simulated.
512 devices in a mesh: dp: 32 (over z_hi, x, core), seq: 16 (over y, z_lo).
Axes of the slice: x: 4, y: 4, z: 16 (z_hi: 4, z_lo: 4; z = z_hi * 4 + z_lo), core: 2. Of those that a mesh axis runs over, the one named last changes fastest.
Arguments:
- section_input: bfloat16 [32, 2048, 768], P('dp', 'seq'), may hold values from -6 to 6
- conv_kernel: bfloat16 [5, 768, 768], P(None, None, 'seq'), may hold values from -0.09375 to 0.09375
- qkv_weight: bfloat16 [1536, 4608], P(None, 'seq'), may hold values from -0.15625 to 0.15625
- gain_in: float32 [768], replicated, may hold values from 0.1 to 1.9
- gain_mid: float32 [1536], replicated, may hold values from 0.1 to 1.9
- qkv_cotangent: bfloat16 [32, 1024, 4608], P('dp', None, 'seq'), may hold values from -6 to 6
Outputs:
- qkv: bfloat16 [32, 1024, 4608], P('dp', None, 'seq')
- input_grad: bfloat16 [32, 2048, 768], P('dp', 'seq')
- kernel_grad: bfloat16 [5, 768, 768], P(None, None, 'seq')
- gain_in_grad: float32 [768], replicated
- gain_mid_grad: float32 [1536], replicated
- weight_grad: bfloat16 [1536, 4608], P(None, 'seq')
All inputs are finite; a program needn't handle non-finite values.
Results may differ from a plain program's by a relative error of at most 0.02.
Values may be sent and summed in bfloat16 or wider, within the bound.
A program may use at most 64 MiB of HBM per device.

v0:
```python
import math

import jax
import jax.numpy as jnp
from jax import lax
from jax.sharding import PartitionSpec as P

EPS = 1e-06


def extended(cells, sides, width):
    for axis, dim in sides:
        count = lax.axis_size(axis)
        ends = count - 1
        head = lax.slice_in_dim(cells, 0, width, axis=dim)
        tail = lax.slice_in_dim(cells, cells.shape[dim] - width, cells.shape[dim], axis=dim)
        cells = jnp.concatenate(
            [
                lax.ppermute(tail, axis, [(i, (i + 1) % count) for i in range(ends)]),
                cells,
                lax.ppermute(head, axis, [((i + 1) % count, i) for i in range(ends)]),
            ],
            axis=dim,
        )
    return cells


def inverse_rms(values):
    return lax.rsqrt(jnp.mean(values * values, axis=-1, keepdims=True) + EPS)


def forward_taps(rows, kernel, length):
    total = jnp.dot(rows[0:length], kernel[0], preferred_element_type=jnp.float32)
    for k in range(1, 5):
        total = total + jnp.dot(rows[k : k + length], kernel[k], preferred_element_type=jnp.float32)
    return total


def backward_taps(total, rows, kernel, length):
    for k in range(5):
        total = total + lax.dot_general(
            rows[4 - k : 4 - k + length],
            kernel[k],
            (((1,), (1,)), ((), ())),
            preferred_element_type=jnp.float32,
        )
    return total


def body(section_input, conv_kernel, qkv_weight, gain_in, gain_mid, qkv_cotangent):
    seq_rows = section_input[0]
    length, chans = seq_rows.shape
    half = length // 2
    width = 2 * chans
    shards = lax.axis_size("seq")
    scale = 1.0 / math.sqrt(lax.axis_size("dp") * shards * half)
    xfull = seq_rows.astype(jnp.float32)
    rone = inverse_rms(xfull)
    aone = xfull * rone
    normed_in = (aone * gain_in).astype(jnp.bfloat16)
    all_in = lax.all_gather(normed_in, "seq", axis=0, tiled=True)
    total_len = all_in.shape[0]
    padded_all = jnp.pad(all_in, ((2, 2), (0, 0)))
    full_kernel = lax.all_gather(conv_kernel, "seq", axis=2, tiled=True)
    own_rows = lax.dynamic_slice_in_dim(padded_all, lax.axis_index("seq") * length, length + 4, 0)
    conv_out = forward_taps(own_rows, full_kernel, length)
    sig = jax.nn.sigmoid(conv_out)
    pooled = (xfull + conv_out * sig).reshape(half, width)
    rtwo = inverse_rms(pooled)
    atwo = pooled * rtwo
    normed_mid = (atwo * gain_mid).astype(jnp.bfloat16)
    grads_out = qkv_cotangent[0]
    all_normed = lax.all_gather(normed_mid, "seq", axis=0, tiled=True)
    qkv_out = jnp.dot(all_normed, qkv_weight, preferred_element_type=jnp.float32).astype(
        jnp.bfloat16
    )
    mid_grad = lax.psum_scatter(
        lax.dot_general(
            grads_out, qkv_weight, (((1,), (1,)), ((), ())), preferred_element_type=jnp.float32
        ).astype(jnp.bfloat16),
        "seq",
        scatter_dimension=0,
        tiled=True,
    ).astype(jnp.float32)
    proj_grad = lax.dot_general(
        all_normed, grads_out, (((0,), (0,)), ((), ())), preferred_element_type=jnp.float32
    )
    gain_mid_term = jnp.sum(mid_grad * atwo, axis=0)
    gmid = gain_mid * mid_grad
    pooled_grad = rtwo * (gmid - atwo * jnp.mean(gmid * atwo, axis=-1, keepdims=True))
    section_grad = pooled_grad.reshape(length, chans)
    conv_grad = (section_grad * sig * (1.0 + conv_out * (1.0 - sig))).astype(jnp.bfloat16)
    grad_pad = extended(conv_grad, (("seq", 0),), 2)
    empty = jnp.zeros((length, chans), jnp.float32)
    normed_grad = backward_taps(empty, grad_pad, full_kernel, length)
    grad_cols = lax.all_to_all(conv_grad, "seq", split_axis=1, concat_axis=0, tiled=True)
    kernel_term = jnp.stack(
        [
            lax.dot_general(
                padded_all[k : k + total_len],
                grad_cols,
                (((0,), (0,)), ((), ())),
                preferred_element_type=jnp.float32,
            )
            for k in range(5)
        ]
    )
    gain_in_term = jnp.sum(normed_grad * aone, axis=0)
    hin = gain_in * normed_grad
    input_grad = (
        section_grad + rone * (hin - aone * jnp.mean(hin * aone, axis=-1, keepdims=True))
    ).astype(jnp.bfloat16)
    kernel_total, proj_total = lax.psum((kernel_term, proj_grad), "dp")
    gain_in_total, gain_mid_total = lax.psum((gain_in_term, gain_mid_term), ("dp", "seq"))
    return (
        qkv_out[None],
        input_grad[None],
        (kernel_total * scale).astype(jnp.bfloat16),
        gain_in_total * scale,
        gain_mid_total * scale,
        (proj_total * scale).astype(jnp.bfloat16),
    )


def solution(mesh):
    placed = (
        P("dp", "seq", None),
        P(None, None, "seq"),
        P(None, "seq"),
        P(),
        P(),
        P("dp", None, "seq"),
    )
    return jax.shard_map(
        body,
        mesh=mesh,
        in_specs=placed,
        out_specs=(
            P("dp", None, "seq"),
            P("dp", "seq", None),
            P(None, None, "seq"),
            P(),
            P(),
            P(None, "seq"),
        ),
        check_vma=False,
    )
```

profile of v0, /device:TPU:1, one launch (start us, length us, event | category | flops | bytes accessed | tf_op | source)
XLA Modules:
  0.0 825.8 jit_solution(18285490777444004254)
XLA Ops:
  7.2 1.1 fusion.59
  8.4 1.7 fusion.52
  10.9 4.5 convolution_convert_fusion
  15.5 87.5 %all-gather.4.cloned.1.call-done = bf16[2048,768]{1,0:T(8,128)(2,1)} async-done(((bf16[128,768]{1,0:T(8,128)(2,1)}), bf16[2048,768]{1,0:T(8,128)(2,1)}) %all-gather.4.cloned.1.call-update) | async-done | bytes 3145744 | tf_op jit(solution)/shard_map/all_gather | solution.py:61
  103.0 149.8 %all-gather.6.cloned.1.call-done = bf16[5,768,768]{1,2,0:T(8,128)(2,1)} async-done(((bf16[5,768,48]{1,2,0:T(8,128)(2,1)}), bf16[5,768,768]{1,2,0:T(8,128)(2,1)}) %all-gather.6.cloned.1.call-update) | async-done | bytes 5898256 | tf_op jit(solution)/shard_map/all_gather | solution.py:64
  252.8 2.1 fusion.36
  255.1 2.5 convolution_add_fusion.5
  260.2 84.0 %reduce-scatter.2.cloned.1.call-done = bf16[64,1536]{1,0:T(8,128)(2,1)} async-done(((bf16[1024,1536]{1,0:T(8,128)(2,1)}), bf16[64,1536]{1,0:T(8,128)(2,1)}) %reduce-scatter.2.cloned.1.call-update) | async-done | bytes 196624 | tf_op jit(solution)/shard_map/reduce_scatter | solution.py:77
  344.2 1.2 fusion.51
  345.4 1.8 fusion.50
  347.4 0.8 copy.12
  348.2 4.0 all-to-all-start
  352.3 1.3 collective-permute-start
  353.6 4.0 collective-permute-start.1
  357.6 2.2 all-to-all-done
  359.8 3.0 fusion.26
  362.8 1.0 fusion.14
  364.5 1.0 fusion.20
  365.5 1.0 fusion.32
  366.4 76.6 %all-gather.8.cloned.1.call-done = bf16[1024,1536]{1,0:T(8,128)(2,1)} async-done(((bf16[64,1536]{1,0:T(8,128)(2,1)}), bf16[1024,1536]{1,0:T(8,128)(2,1)}) %all-gather.8.cloned.1.call-update) | async-done | bytes 3145744 | tf_op jit(solution)/shard_map/all_gather | solution.py:73
  443.1 4.3 fusion.44
  447.3 1.6 fusion.38
  449.0 1.6 fusion.39
  450.6 1.6 fusion.37
  452.2 1.6 fusion.9
  453.8 1.7 fusion.58
  455.5 112.6 %all-reduce.1 = (f32[768]{0:T(1024)S(1)}, f32[1536]{0:T(1024)S(1)}) all-reduce(f32[768]{0:T(1024)S(1)} %get-tuple-element.8, f32[1536]{0:T(1024)S(1)} %get-tuple-element.6), channel_id=1, replica_groups=mesh['dp'=32,'seq'=16] {'dp','seq'}, use_global_device_ids=true, to_apply=%region_8.9 | all-reduce | flops 2304 | bytes 18432 | tf_op jit(solution)/shard_map/psum | solution.py:114
  569.3 0.9 fusion.68
  570.2 3.8 fusion.8
  574.0 240.8 %all-reduce.5.cloned.1.call-done = (f32[5,768,48]{1,2,0:T(8,128)}, f32[1536,288]{0,1:T(8,128)}) async-done(((f32[5,768,48]{1,2,0:T(8,128)}, f32[1536,288]{0,1:T(8,128)}), (f32[5,768,48]{1,2,0:T(8,128)}, f32[1536,288]{0,1:T(8,128)})) %all-reduce.5.cloned.1.call-update) | async-done | bytes 2506768 | tf_op jit(solution)/shard_map/psum | solution.py:113
  814.9 1.9 multiply_convert_fusion.1
  816.8 2.5 multiply_convert_fusion
  (46 shorter events, 5.9 us)
Async XLA Ops:
  7.2 3.7 copy-start
  7.2 95.8 %all-gather.4.cloned.1.call-start = ((), (), s32[]{:S(2)}) async-start(), calls=%async_computation.2 | async-start | bytes 3342336 | tf_op jit(solution)/shard_map/all_gather | solution.py:61
  10.1 242.7 %all-gather.6.cloned.1.call-start = ((), (), s32[]{:S(2)}) async-start(), calls=%async_computation.3 | async-start | bytes 6266880 | tf_op jit(solution)/shard_map/all_gather | solution.py:64
  10.9 333.3 %reduce-scatter.2.cloned.1.call-start = ((), (), s32[]{:S(2)}) async-start(), calls=%async_computation.5 | async-start | bytes 3342336 | tf_op jit(solution)/shard_map/reduce_scatter | solution.py:77
  15.5 427.6 %all-gather.8.cloned.1.call-start = ((), (), s32[]{:S(2)}) async-start(), calls=%async_computation.4 | async-start | bytes 3342336 | tf_op jit(solution)/shard_map/all_gather | solution.py:73
  252.8 2.3 copy-start.1
  252.8 4.9 copy-start.3
  258.2 0.9 copy-start.4
  259.2 85.0 %copy-start.6 = (f32[1536]{0:T(1024)S(1)}, f32[1536]{0:T(1024)}, u32[]{:S(2)}) copy-start(f32[1536]{0:T(1024)} %param.10) | copy-start | bytes 18436
  348.2 11.5 %all-to-all-start = ((bf16[128,16,48]{0,2,1:T(8,128)(2,1)}), bf16[128,16,48]{0,2,1:T(8,128)(2,1)S(1)}, u32[]{:S(2)}, u32[]{:S(2)}) async-start(bf16[128,16,48]{0,2,1:T(8,128)(2,1)} %bitcast.10), calls=%async_computation.1 | async-start | bytes 393216 | tf_op jit(solution)/shard_map/all_to_all | solution.py:96
  352.3 462.6 %all-reduce.5.cloned.1.call-start = ((), (), s32[]{:S(2)}) async-start(), calls=%async_computation.6 | async-start | bytes 5013504 | tf_op jit(solution)/shard_map/psum | solution.py:113
  352.3 98.3 %collective-permute-start = (bf16[2,768]{1,0:T(2,128)(2,1)S(1)}, bf16[2,768]{1,0:T(2,128)(2,1)S(1)}, u32[]{:S(2)}, u32[]{:S(2)}) collective-permute-start(bf16[2,768]{1,0:T(2,128)(2,1)S(1)} %get-tuple-element.18), channel_id=1, source_target_pairs={{1,0},{2,1},{3,2},{4,3},{5,4},{6,5},{7,6},{8,7},{9,8},{10,9},{11,1... | collective-permute-start | bytes 9224 | tf_op jit(solution)/shard_map/ppermute | solution.py:21
  353.6 95.3 %collective-permute-start.1 = (bf16[2,768]{1,0:T(2,128)(2,1)S(1)}, bf16[2,768]{1,0:T(2,128)(2,1)S(1)}, u32[]{:S(2)}, u32[]{:S(2)}) collective-permute-start(bf16[2,768]{1,0:T(2,128)(2,1)S(1)} %get-tuple-element.19), channel_id=1, source_target_pairs={{0,1},{1,2},{2,3},{3,4},{4,5},{5,6},{6,7},{7,8},{8,9},{9,10},{10,1... | collective-permute-start | bytes 9224 | tf_op jit(solution)/shard_map/ppermute | solution.py:19
  359.8 3.0 copy-start.2
  364.5 78.6 %copy-start.8 = (bf16[1,1024,288]{1,2,0:T(8,128)(2,1)S(1)}, bf16[1,1024,288]{1,2,0:T(8,128)(2,1)}, u32[]{:S(2)}) copy-start(bf16[1,1024,288]{1,2,0:T(8,128)(2,1)} %param.11) | copy-start | bytes 1769476
  366.4 80.9 %copy-start.5 = (f32[5,768,48]{1,2,0:T(8,128)}, f32[5,768,48]{1,2,0:T(8,128)S(1)}, u32[]{:S(2)}) copy-start(f32[5,768,48]{1,2,0:T(8,128)S(1)} %fusion.32) | copy-start | bytes 2211844
  449.0 4.9 copy-start.7
Sparse Core Ops, SparseCore 0:
  10.6 92.2 all-gather.3
  105.1 147.6 all-gather.5
  255.6 88.5 reduce-scatter.1
  347.3 95.6 all-gather.7
  447.5 367.3 all-reduce.4
where the time goes:
time: 829 us; the launch traced here: 826 us
  waiting for transfers between devices  642 us (77%)
  blocking collectives  113 us (14%)
  matrix products  33.7 us (4%)
  between operations  14 us (2%)
  other arithmetic  12.6 us (2%)
  starting transfers between devices  9.49 us (1%)
    psum x1, waiting for transfers between devices, body(): kernel_total, proj_total = lax.psum((kernel_term, proj_grad), 'dp')  241 us
    all_gather x1, waiting for transfers between devices, body(): full_kernel = lax.all_gather(conv_kernel, 'seq', axis=2, tiled=True)  150 us
    psum x1, blocking collectives, body(): lax.psum((gain_in_term, gain_mid_term), ('dp', 'seq'))  113 us
    all_gather x1, waiting for transfers between devices, body(): all_in = lax.all_gather(normed_in, 'seq', axis=0, tiled=True)  87.5 us
    reduce_scatter x1, waiting for transfers between devices, body(): lax.psum_scatter(lax.dot_general(grads_out, qkv_weight, (((1,), (1,)), ((...  84 us
    all_gather x1, waiting for transfers between devices, body(): all_normed = lax.all_gather(normed_mid, 'seq', axis=0, tiled=True)  76.6 us
  transfers between devices with their start and end apart: 8, of which 6 were waited for; matrix products, arithmetic and copies ran while one was open for 5% of the time, Pallas kernels for 0%

commit v1 on v0

v1 whole, which is shorter than its diff:
```python
import functools
import math

import jax
import jax.numpy as jnp
from jax import lax
from jax.experimental import pallas as pl
from jax.experimental.pallas import tpu as pltpu
from jax.sharding import PartitionSpec as P

EPS = 1e-06
MESH = pl.DeviceIdType.MESH
F32 = jnp.float32
BF16 = jnp.bfloat16


def wrap4(i):
    return lax.rem(i + 8, 4)


class Place:
    def __init__(self):
        self.dp = lax.axis_index("dp")
        self.seq = lax.axis_index("seq")
        self.z_hi = self.dp // 8
        self.x = lax.rem(self.dp // 2, 4)
        self.core = lax.rem(self.dp, 2)
        self.y = self.seq // 4
        self.z = lax.rem(self.seq, 4)

    def at_seq(self, y, z):
        return (self.dp, y * 4 + z)

    def y_peer(self, step):
        return self.at_seq(wrap4(self.y + step), self.z)

    def z_peer(self, step):
        return self.at_seq(self.y, wrap4(self.z + step))

    def x_peer(self, step):
        return (self.z_hi * 8 + wrap4(self.x + step) * 2 + self.core, self.seq)

    def z_hi_peer(self, step):
        return (wrap4(self.z_hi + step) * 8 + self.x * 2 + self.core, self.seq)

    def other_core(self):
        return (self.z_hi * 8 + self.x * 2 + 1 - self.core, self.seq)


class Wire:
    def __init__(self, send_sems, recv_sems, anyone):
        self.send_sems = send_sems
        self.recv_sems = recv_sems
        self.anyone = anyone
        self.started = []
        self.names = {}

    def number(self, name):
        return self.names.setdefault(name, len(self.names))

    def send(self, name, src, dst, device):
        k = self.number(name)
        copy = pltpu.make_async_remote_copy(
            src_ref=src,
            dst_ref=dst,
            send_sem=self.send_sems.at[k],
            recv_sem=self.recv_sems.at[k],
            device_id=device,
            device_id_type=MESH,
        )
        copy.start()
        self.started.append(copy)

    def recv(self, name, ref):
        k = self.number(name)
        pltpu.make_async_remote_copy(
            src_ref=ref,
            dst_ref=ref,
            send_sem=self.send_sems.at[k],
            recv_sem=self.recv_sems.at[k],
            device_id=self.anyone,
            device_id_type=MESH,
        ).wait_recv()

    def drain(self):
        for copy in self.started:
            copy.wait_send()


def greet(peers):
    barrier = pltpu.get_barrier_semaphore()
    for peer in peers:
        pl.semaphore_signal(barrier, inc=1, device_id=peer, device_id_type=MESH)
    pl.semaphore_wait(barrier, len(peers))


class Gather:
    def __init__(self, wire, place, tag, view):
        self.wire, self.place, self.tag, self.view = wire, place, tag, view

    def column(self, step):
        return self.view(wrap4(self.place.y + step) * 4, 4)

    def start(self, src):
        p = self.place
        for d in (1, 3, 2):
            self.wire.send((self.tag, "z", d), src, self.view(p.seq, 1), p.z_peer(d))

    def own_column(self):
        p = self.place
        for d in (1, 3, 2):
            block = p.y * 4 + wrap4(p.z - d)
            self.wire.recv((self.tag, "z", d), self.view(block, 1))
        for step in (1, -1):
            mine = self.column(0)
            self.wire.send((self.tag, "y", step), mine, mine, p.y_peer(step))

    def near_columns(self):
        p = self.place
        for step, skip in ((1, 0), (-1, 2)):
            got = self.column(-step)
            self.wire.recv((self.tag, "y", step), got)
            part = self.view(wrap4(p.y - step) * 4 + skip, 2)
            self.wire.send((self.tag, "relay", step), part, part, p.y_peer(step))

    def far_column(self):
        far = wrap4(self.place.y + 2) * 4
        for step, skip in ((1, 0), (-1, 2)):
            self.wire.recv((self.tag, "relay", step), self.view(far + skip, 2))


def first_kernel(
    rows_ref, taps_ref, wt_ref, cot_ref, all_rows_ref, all_taps_ref, mid_ref,
    sums, far_send, far_recv, near_send, near_recv, column_ref, z_recv,
    send_sems, recv_sems, local_sems,
):
    p = Place()
    wire = Wire(send_sems, recv_sems, p.other_core())
    greet(
        [p.z_peer(d) for d in (1, 2, 3)]
        + [p.y_peer(1), p.y_peer(-1), p.x_peer(1), p.x_peer(-1), p.other_core()]
    )
    chans = rows_ref.shape[1]
    lanes_half = chans // 2
    lanes = pl.ds(pl.multiple_of(p.core * lanes_half, 128), lanes_half)
    tap_rows = taps_ref.shape[0]
    quarter = tap_rows // 4

    def piece_rows(x):
        return pl.ds(pl.multiple_of(x * quarter, 16), quarter)

    def taps_view(first, count):
        return all_taps_ref.at[pl.ds(first, count), piece_rows(p.x), lanes]

    def rows_view(first, count):
        return all_rows_ref.at[pl.ds(first, count)]

    taps = Gather(wire, p, "taps", taps_view)
    rows = Gather(wire, p, "rows", rows_view)
    own_taps = taps_ref.at[piece_rows(p.x), lanes]
    own_rows = rows_ref
    copies = [
        pltpu.make_async_copy(own_taps, all_taps_ref.at[p.seq, piece_rows(p.x), lanes], local_sems.at[0]),
        pltpu.make_async_copy(own_rows, all_rows_ref.at[p.seq], local_sems.at[1]),
    ]
    for d in (1, 3, 2):
        wire.send(("taps", "z", d), own_taps, all_taps_ref.at[p.seq, piece_rows(p.x), lanes], p.z_peer(d))
    for copy in copies:
        copy.start()

    length = cot_ref.shape[1] // 4
    half = length // 2
    width = wt_ref.shape[1]
    tile = 256

    def product(step, slot):
        cols = pl.ds(pl.multiple_of(wrap4(p.y + step) * length, 128), length)
        part = cot_ref[:, cols].T

        @pl.loop(0, width // tile)
        def _(n):
            span = pl.ds(pl.multiple_of(n * tile, tile), tile)
            sums[slot, :, span] = jnp.dot(part, wt_ref[:, span], preferred_element_type=F32)

    for copy in copies:
        copy.wait()
    product(2, 0)
    far_send[...] = sums[0].astype(BF16)
    wire.send("far+", far_send.at[pl.ds(0, half)], far_recv.at[0], p.y_peer(1))
    wire.send("far-", far_send.at[pl.ds(half, half)], far_recv.at[1], p.y_peer(-1))
    for d in (1, 3, 2):
        wire.send(("rows", "z", d), own_rows, all_rows_ref.at[p.seq], p.z_peer(d))
    taps.own_column()

    def x_send(step, column):
        part = taps.column(column)
        for way in (1, -1):
            wire.send(("x", way, column), part, part, p.x_peer(way))

    x_send(0, 0)
    product(1, 1)
    product(-1, 2)
    wire.recv("far+", far_recv.at[0])
    near_send[0, :half] = (sums[1, :half] + far_recv[0].astype(F32)).astype(BF16)
    near_send[0, half:] = sums[1, half:].astype(BF16)
    wire.send("near+", near_send.at[0], near_recv.at[0], p.y_peer(1))
    wire.recv("far-", far_recv.at[1])
    near_send[1, :half] = sums[2, :half].astype(BF16)
    near_send[1, half:] = (sums[2, half:] + far_recv[1].astype(F32)).astype(BF16)
    wire.send("near-", near_send.at[1], near_recv.at[1], p.y_peer(-1))
    taps.near_columns()
    x_send(0, 1)
    x_send(0, -1)
    rows.own_column()
    product(0, 0)
    taps.far_column()
    x_send(0, 2)

    def x_part(x, column):
        first = wrap4(p.y + column) * 4
        return all_taps_ref.at[pl.ds(first, 4), piece_rows(x), lanes]

    for column in (0, 1, -1, 2):
        for way in (1, -1):
            got = x_part(wrap4(p.x - way), column)
            wire.recv(("x", way, column), got)
            if (way == 1) == (column in (0, 1)):
                wire.send(("xx", column), got, got, p.x_peer(way))

    wire.recv("near+", near_recv.at[0])
    wire.recv("near-", near_recv.at[1])
    sums[0] = sums[0] + near_recv[0].astype(F32) + near_recv[1].astype(F32)
    column_ref[...] = sums[0].astype(BF16).reshape(column_ref.shape)
    for d in (1, 3, 2):
        to = wrap4(p.z + d)
        wire.send(("mid", d), column_ref.at[to], z_recv.at[d - 1], p.z_peer(d))

    def core_part(core, column):
        first = wrap4(p.y + column) * 4
        half_lanes = pl.ds(pl.multiple_of(core * lanes_half, 128), lanes_half)
        return all_taps_ref.at[pl.ds(first, 4), :, half_lanes]

    for column in (0, 1, -1, 2):
        wire.recv(("xx", column), x_part(wrap4(p.x + 2), column))
        part = core_part(p.core, column)
        wire.send(("core", column), part, part, p.other_core())
    rows.near_columns()
    for d in (1, 3, 2):
        wire.recv(("mid", d), z_recv.at[d - 1])
    block = mid_ref.shape[0]
    own = sums[0, pl.ds(pl.multiple_of(p.z * block, 8), block), :]
    mid_ref[...] = own + z_recv[0].astype(F32) + z_recv[1].astype(F32) + z_recv[2].astype(F32)
    for column in (0, 1, -1, 2):
        wire.recv(("core", column), core_part(1 - p.core, column))
    rows.far_column()
    wire.drain()


def first_call(rows, taps, wt, cot):
    shards = lax.axis_size("seq")
    length, chans = rows.shape
    width = wt.shape[1]
    column = cot.shape[1] // 4
    block = cot.shape[1] // shards
    vmem = pl.BlockSpec(memory_space=pltpu.VMEM)
    return pl.pallas_call(
        first_kernel,
        name="first",
        out_shape=(
            jax.ShapeDtypeStruct((shards, length, chans), BF16),
            jax.ShapeDtypeStruct((shards,) + taps.shape, BF16),
            jax.ShapeDtypeStruct((block, width), F32),
        ),
        in_specs=[vmem] * 4,
        out_specs=(vmem,) * 3,
        scratch_shapes=[
            pltpu.VMEM((3, column, width), F32),
            pltpu.VMEM((column, width), BF16),
            pltpu.VMEM((2, column // 2, width), BF16),
            pltpu.VMEM((2, column, width), BF16),
            pltpu.VMEM((2, column, width), BF16),
            pltpu.VMEM((4, block, width), BF16),
            pltpu.VMEM((3, block, width), BF16),
            pltpu.SemaphoreType.DMA((48,)),
            pltpu.SemaphoreType.DMA((48,)),
            pltpu.SemaphoreType.DMA((2,)),
        ],
        compiler_params=pltpu.CompilerParams(collective_id=0, has_side_effects=True, vmem_limit_bytes=60 << 20),
    )(rows, taps, wt, cot)


def second_kernel(
    mid_ref, cols_ref, head_ref, tail_ref, all_mid_ref, all_cols_ref, before_ref, after_ref,
    send_sems, recv_sems, local_sems,
):
    p = Place()
    wire = Wire(send_sems, recv_sems, p.other_core())
    shards = all_mid_ref.shape[0]

    def seq_peer(d):
        return (p.dp, lax.rem(p.seq + d, shards))

    greet([seq_peer(d) for d in range(1, shards)])
    mid = Gather(wire, p, "mid", lambda first, count: all_mid_ref.at[pl.ds(first, count)])
    for d in (1, 3, 2):
        wire.send(("mid", "z", d), mid_ref, all_mid_ref.at[p.seq], p.z_peer(d))
    own = cols_ref.shape[0] // shards

    def owned(j):
        return cols_ref.at[pl.ds(pl.multiple_of(j * own, 16), own)]

    copies = [
        pltpu.make_async_copy(mid_ref, all_mid_ref.at[p.seq], local_sems.at[0]),
        pltpu.make_async_copy(owned(p.seq), all_cols_ref.at[p.seq], local_sems.at[1]),
    ]
    for copy in copies:
        copy.start()
    wire.send("tail", tail_ref, before_ref, seq_peer(1))
    wire.send("head", head_ref, after_ref, seq_peer(shards - 1))
    for d in range(1, shards):
        wire.send(("cols", d), owned(lax.rem(p.seq + d, shards)), all_cols_ref.at[p.seq], seq_peer(d))
    for copy in copies:
        copy.wait()
    mid.own_column()
    mid.near_columns()
    wire.recv("tail", before_ref)
    wire.recv("head", after_ref)
    for d in range(1, shards):
        wire.recv(("cols", d), all_cols_ref.at[lax.rem(p.seq + shards - d, shards)])
    mid.far_column()
    wire.drain()


def second_call(mid, cols, head, tail):
    shards = lax.axis_size("seq")
    vmem = pl.BlockSpec(memory_space=pltpu.VMEM)
    return pl.pallas_call(
        second_kernel,
        name="second",
        out_shape=(
            jax.ShapeDtypeStruct((shards,) + mid.shape, BF16),
            jax.ShapeDtypeStruct((shards, cols.shape[0] // shards, cols.shape[1]), BF16),
            jax.ShapeDtypeStruct(head.shape, BF16),
            jax.ShapeDtypeStruct(head.shape, BF16),
        ),
        in_specs=[vmem] * 4,
        out_specs=(vmem,) * 4,
        scratch_shapes=[
            pltpu.SemaphoreType.DMA((26,)),
            pltpu.SemaphoreType.DMA((26,)),
            pltpu.SemaphoreType.DMA((2,)),
        ],
        compiler_params=pltpu.CompilerParams(collective_id=1, has_side_effects=True),
    )(mid, cols, head, tail)


def third_kernel(
    scale, sums_ref, gain_ref, out_ref, gain_out_ref,
    core_recv, core_sum, x_recv, x_sum, z_recv, gain_core, gain_send, gain_recv,
    send_sems, recv_sems,
):
    p = Place()
    wire = Wire(send_sems, recv_sems, p.other_core())
    stages = (p.x_peer, p.z_hi_peer, p.z_peer, p.y_peer)
    ways = (1, 3, 2)
    greet([p.other_core()] + [peer(d) for peer in stages for d in ways])

    wire.send("gain", gain_ref, gain_core, p.other_core())
    wire.send("core", sums_ref.at[1 - p.core], core_recv, p.other_core())

    def gain_stage(stage):
        for d in ways:
            wire.send(("gain", stage, d), gain_send.at[stage], gain_recv.at[stage, d - 1], stages[stage](d))

    def gain_sum(stage):
        total = gain_send[stage]
        for d in ways:
            wire.recv(("gain", stage, d), gain_recv.at[stage, d - 1])
            total = total + gain_recv[stage, d - 1]
        return total

    wire.recv("gain", gain_core)
    gain_send[0] = gain_ref[...] + gain_core[...]
    gain_stage(0)
    wire.recv("core", core_recv)

    def add_core(x):
        core_sum[x] = (sums_ref[p.core, x].astype(F32) + core_recv[x].astype(F32)).astype(BF16)

    for d in ways:
        to = wrap4(p.x + d)
        add_core(to)
        wire.send(("x", d), core_sum.at[to], x_recv.at[d - 1], p.x_peer(d))
    add_core(p.x)
    gain_send[1] = gain_sum(0)
    gain_stage(1)
    for d in ways:
        wire.recv(("x", d), x_recv.at[d - 1])

    def add_x(z):
        total = core_sum[p.x, z].astype(F32)
        for d in ways:
            total = total + x_recv[d - 1, z].astype(F32)
        x_sum[z] = total.astype(BF16)

    for d in (2, 1, 3):
        to = wrap4(p.z_hi + d)
        add_x(to)
        wire.send(("z", d), x_sum.at[to], z_recv.at[d - 1], p.z_hi_peer(d))
    add_x(p.z_hi)
    gain_send[2] = gain_sum(1)
    gain_stage(2)
    total = x_sum[p.z_hi].astype(F32)
    for d in ways:
        wire.recv(("z", d), z_recv.at[d - 1])
        total = total + z_recv[d - 1].astype(F32)
    out_ref[p.core, p.x, p.z_hi] = (total * scale).astype(BF16)
    mine = out_ref.at[p.core, p.x, p.z_hi]
    for d in (2, 1, 3):
        wire.send(("zz", d), mine, mine, p.z_hi_peer(d))
    gain_send[3] = gain_sum(2)
    gain_stage(3)
    for d in (1, 3, 2):
        wire.recv(("zz", d), out_ref.at[p.core, p.x, wrap4(p.z_hi - d)])
    mine = out_ref.at[p.core, p.x]
    for d in ways:
        wire.send(("xx", d), mine, mine, p.x_peer(d))
    gain_out_ref[...] = gain_sum(3) * scale
    for d in ways:
        wire.recv(("xx", d), out_ref.at[p.core, wrap4(p.x - d)])
    mine = out_ref.at[p.core]
    wire.send("cc", mine, mine, p.other_core())
    wire.recv("cc", out_ref.at[1 - p.core])
    wire.drain()


def third_call(scale, sums, gains):
    vmem = pl.BlockSpec(memory_space=pltpu.VMEM)
    blocks = sums.shape[1:]
    return pl.pallas_call(
        functools.partial(third_kernel, scale),
        name="third",
        out_shape=(
            jax.ShapeDtypeStruct(sums.shape, BF16),
            jax.ShapeDtypeStruct(gains.shape, F32),
        ),
        in_specs=[vmem] * 2,
        out_specs=(vmem,) * 2,
        scratch_shapes=[
            pltpu.VMEM(blocks, BF16),
            pltpu.VMEM(blocks, BF16),
            pltpu.VMEM((3,) + blocks[1:], BF16),
            pltpu.VMEM(blocks[1:], BF16),
            pltpu.VMEM((3,) + blocks[2:], BF16),
            pltpu.VMEM(gains.shape, F32),
            pltpu.VMEM((4,) + gains.shape, F32),
            pltpu.VMEM((4, 3) + gains.shape, F32),
            pltpu.SemaphoreType.DMA((27,)),
            pltpu.SemaphoreType.DMA((27,)),
        ],
        compiler_params=pltpu.CompilerParams(collective_id=2, has_side_effects=True),
    )(sums, gains)


def inverse_rms(values):
    return lax.rsqrt(jnp.mean(values * values, axis=-1, keepdims=True) + EPS)


def contract(a, b, dims):
    return lax.dot_general(a, b, (dims, ((), ())), preferred_element_type=F32)


def body(section_input, conv_kernel, qkv_weight, gain_in, gain_mid, qkv_cotangent):
    seq_rows = section_input[0]
    length, chans = seq_rows.shape
    half = length // 2
    width = 2 * chans
    shards = lax.axis_size("seq")
    seq = lax.axis_index("seq")
    own = conv_kernel.shape[2]
    scale = 1.0 / math.sqrt(lax.axis_size("dp") * shards * half)
    wt = qkv_weight.T
    cot = qkv_cotangent[0].T
    taps = jnp.transpose(conv_kernel, (0, 2, 1)).reshape(5 * own, chans)
    taps = jnp.pad(taps, ((0, -(5 * own) % 64), (0, 0)))

    xfull = seq_rows.astype(F32)
    rone = inverse_rms(xfull)
    aone = xfull * rone
    normed_in = (aone * gain_in).astype(BF16)
    all_in, all_taps, mid_grad = first_call(normed_in, taps, wt, cot)
    all_in = all_in.reshape(shards * length, chans)
    full = [
        all_taps[:, k * own : (k + 1) * own].reshape(chans, chans) for k in range(5)
    ]
    padded_all = jnp.pad(all_in, ((2, 2), (0, 0)))
    rows = lax.dynamic_slice_in_dim(padded_all, seq * length, length + 4, 0)
    conv_out = sum(contract(rows[k : k + length], full[k], ((1,), (1,))) for k in range(5))
    sig = jax.nn.sigmoid(conv_out)
    pooled = (xfull + conv_out * sig).reshape(half, width)
    rtwo = inverse_rms(pooled)
    atwo = pooled * rtwo
    normed_mid = (atwo * gain_mid).astype(BF16)
    gain_mid_term = jnp.sum(mid_grad * atwo, axis=0)
    gmid = gain_mid * mid_grad
    pooled_grad = rtwo * (gmid - atwo * jnp.mean(gmid * atwo, axis=-1, keepdims=True))
    section_grad = pooled_grad.reshape(length, chans)
    conv_grad = (section_grad * sig * (1.0 + conv_out * (1.0 - sig))).astype(BF16)
    all_mid, grad_cols, before, after = second_call(
        normed_mid, conv_grad.T, conv_grad[:16], conv_grad[length - 16 :]
    )
    all_mid = all_mid.reshape(shards * half, width)
    qkv_t = contract(wt, all_mid, ((1,), (1,))).astype(BF16)
    proj_t = contract(cot, all_mid, ((1,), (0,)))

    before = jnp.where(seq > 0, before[14:], jnp.zeros((2, chans), BF16))
    after = jnp.where(seq < shards - 1, after[:2], jnp.zeros((2, chans), BF16))
    grad_pad = jnp.concatenate([before, conv_grad, after], axis=0)
    normed_grad = sum(
        contract(grad_pad[4 - k : 4 - k + length], full[k], ((1,), (0,))) for k in range(5)
    )
    total = shards * length
    grad_cols = jnp.transpose(grad_cols, (1, 0, 2)).reshape(own, total)
    cols_pad = jnp.pad(grad_cols, ((0, 0), (2, 2)))
    shifted = jnp.concatenate([cols_pad[:, 4 - k : 4 - k + total] for k in range(5)], axis=0)
    kernel_t = contract(shifted, all_in, ((1,), (0,)))
    gain_in_term = jnp.sum(normed_grad * aone, axis=0)
    hin = gain_in * normed_grad
    input_grad = (
        section_grad + rone * (hin - aone * jnp.mean(hin * aone, axis=-1, keepdims=True))
    ).astype(BF16)

    lanes = 256
    parts = [kernel_t[:, i : i + lanes] for i in range(0, chans, lanes)]
    parts += [proj_t[:, i : i + lanes] for i in range(0, width, lanes)]
    used = sum(part.shape[0] for part in parts)
    block = -(-used // (32 * 16)) * 16
    parts.append(jnp.zeros((32 * block - used, lanes), F32))
    packed = jnp.concatenate(parts, axis=0).astype(BF16).reshape(2, 4, 4, block, lanes)
    gains = jnp.concatenate([gain_in_term, gain_mid_term]).reshape(-1, 128)
    gains = jnp.pad(gains, ((0, -gains.shape[0] % 8), (0, 0)))
    packed, gains = third_call(scale, packed, gains)
    packed = packed.reshape(32 * block, lanes)
    kernel_rows = kernel_t.shape[0]
    kernel_total = jnp.concatenate(
        [packed[i * kernel_rows : (i + 1) * kernel_rows] for i in range(chans // lanes)], axis=1
    )
    packed = packed[chans // lanes * kernel_rows :]
    proj_rows = proj_t.shape[0]
    proj_total = jnp.concatenate(
        [packed[i * proj_rows : (i + 1) * proj_rows] for i in range(width // lanes)], axis=1
    )
    gains = gains.reshape(-1)
    return (
        qkv_t.T[None],
        input_grad[None],
        jnp.transpose(kernel_total.reshape(5, own, chans), (0, 2, 1)),
        gains[:chans],
        gains[chans : chans + width],
        proj_total.T,
    )


def solution(mesh):
    placed = (
        P("dp", "seq", None),
        P(None, None, "seq"),
        P(None, "seq"),
        P(),
        P(),
        P("dp", None, "seq"),
    )
    return jax.shard_map(
        body,
        mesh=mesh,
        in_specs=placed,
        out_specs=(
            P("dp", None, "seq"),
            P("dp", "seq", None),
            P(None, None, "seq"),
            P(),
            P(),
            P(None, "seq"),
        ),
        check_vma=False,
    )
```

time: 829 us -> 239 us (0.29)
  waiting for transfers between devices: 642 us -> 0 us
  Pallas kernels: 0 us -> 185 us
  blocking collectives: 113 us -> 0 us
  local copies, waits for them, and re-layouts: 1.83 us -> 21 us
  between operations: 14 us -> 1.04 us
  matrix products: 33.7 us -> 21.6 us
  starting transfers between devices: 9.49 us -> 0 us
    all_gather x3 -> x0, waiting for transfers between devices: 314 us -> none  [the longest x1 150 us: body(): full_kernel = lax.all_gather(conv_kernel, 'seq', axis=2, tiled=True)]
    psum x1 -> x0, waiting for transfers between devices: 241 us -> none  [body(): kernel_total, proj_total = lax.psum((kernel_term, proj_grad), 'dp')]
    pallas_call x0 -> x3, Pallas kernels: none -> 185 us  [the longest x1 74 us: first_call(): pl.pallas_call(first_kernel, name='first', out_shape=(jax.ShapeDtypeStruc...]
    psum x1 -> x0, blocking collectives: 113 us -> none  [body(): lax.psum((gain_in_term, gain_mid_term), ('dp', 'seq'))]
    reduce_scatter x1 -> x0, waiting for transfers between devices: 84 us -> none  [body(): lax.psum_scatter(lax.dot_general(grads_out, qkv_weight, (((1,), (1,)), ((...]
    dot_general x18 -> x13, matrix products: 33.7 us -> 21.6 us  [contract(): return lax.dot_general(a, b, (dims, ((), ())), preferred_element_type=F32)]
    slice x1 -> x5, local copies, waits for them, and re-layouts: 0.01 us -> 8.41 us  [the longest x1 5.45 us: body(): all_taps[:, k * own:(k + 1) * own].reshape(chans, chans)]
  transfers between devices with their start and end apart: 8 -> 0, of which waited for: 6 -> 0; matrix products, arithmetic and copies ran while one was open for 5% -> 0% of each run, Pallas kernels for 0% -> 0%
where the time goes in v1:
time: 239 us
  Pallas kernels  185 us (77%)
  matrix products  21.6 us (9%)
  local copies, waits for them, and re-layouts  21 us (9%)
  other arithmetic  10.1 us (4%)
    pallas_call x1, Pallas kernels, first_call(): pl.pallas_call(first_kernel, name='first', out_shape=(jax.ShapeDtypeStruc...  74 us
    pallas_call x1, Pallas kernels, third_call(): pl.pallas_call(functools.partial(third_kernel, scale), name='third', out_...  56.5 us
    pallas_call x1, Pallas kernels, second_call(): pl.pallas_call(second_kernel, name='second', out_shape=(jax.ShapeDtypeStr...  54.4 us
    dot_general x13, matrix products, contract(): return lax.dot_general(a, b, (dims, ((), ())), preferred_element_type=F32)  21.6 us
    slice x1, local copies, waits for them, and re-layouts, body(): all_taps[:, k * own:(k + 1) * own].reshape(chans, chans)  5.45 us
    unnamed x50, local copies, waits for them, and re-layouts  5.44 us

profile of v1, /device:TPU:1, one launch (start us, length us, event | category | flops | bytes accessed | tf_op | source)
XLA Modules:
  0.0 238.7 jit_solution(10387238148885318460)
XLA Ops:
  0.6 1.0 fusion.14
  1.7 1.7 fusion.7.rows_ref
  3.4 1.8 pad.16.taps_ref
  5.2 74.0 %first.1 = (bf16[16,128,768]{2,1,0:T(8,128)(2,1)}, bf16[16,256,768]{2,1,0:T(8,128)(2,1)}, f32[64,1536]{1,0:T(8,128)}) custom-call(bf16[128,768]{1,0:T(8,128)(2,1)} %fusion.7.rows_ref, bf16[256,768]{1,0:T(8,128)(2,1)} %pad.16.taps_ref, bf16[288,1536]{1,0:T(8,128)(2,1)} %bitcast.95, bf16[288,1024]{1,0:T(8,128)(2,1)} %bitcast.96), custom_call_target="tpu_custom_call" | custom-call | tf_op jit(solution)/shard_map/first/pallas_call | solution.py:266
  79.2 5.4 %fusion.38 = (bf16[16,48,768]{2,1,0:T(8,128)(2,1)}, bf16[16,48,768]{2,1,0:T(8,128)(2,1)}, bf16[16,48,768]{2,1,0:T(8,128)(2,1)}, bf16[16,48,768]{2,1,0:T(8,128)(2,1)}, bf16[16,48,768]{2,1,0:T(8,128)(2,1)}) fusion(bf16[16,256,768]{2,1,0:T(8,128)(2,1)} %get-tuple-element.16), kind=kLoop, calls=%fused_computation.100 | loop fusion | bytes 11796480 | tf_op jit(solution)/shard_map/slice | solution.py:494
  84.7 1.8 fusion.15
  86.5 2.6 %convolution_add_fusion.7 = f32[128,768]{1,0:T(8,128)} fusion(f32[128,768]{1,0:T(8,128)S(1)} %fusion.15, bf16[768,768]{1,0:T(8,128)(2,1)} %bitcast.84, s32[]{:T(128)S(6)} %add.86, bf16[2048,768]{1,0:T(8,128)(2,1)S(1)} %bitcast.71), kind=kOutput, calls=%fused_computation.17 | convolution fusion | flops 151093248 | bytes 5111812 | tf_op jit(solution)/shard_map/dot_general | solution.py:470
  89.0 2.6 %convolution_add_fusion.6 = f32[128,768]{1,0:T(8,128)} fusion(f32[128,768]{1,0:T(8,128)} %convolution_add_fusion.7, bf16[768,768]{1,0:T(8,128)(2,1)} %bitcast.82, s32[]{:T(128)S(6)} %add.87, bf16[2048,768]{1,0:T(8,128)(2,1)S(1)} %bitcast.72), kind=kOutput, calls=%fused_computation.16 | convolution fusion | flops 151093248 | bytes 5111812 | tf_op jit(solution)/shard_map/dot_general | solution.py:470
  91.7 2.7 %convolution_add_fusion.5 = f32[128,768]{1,0:T(8,128)} fusion(f32[128,768]{1,0:T(8,128)} %convolution_add_fusion.6, bf16[768,768]{1,0:T(8,128)(2,1)} %bitcast.80, s32[]{:T(128)S(6)} %add.88, bf16[2048,768]{1,0:T(8,128)(2,1)S(1)} %bitcast.73), kind=kOutput, calls=%fused_computation.15 | convolution fusion | flops 151093248 | bytes 5111812 | tf_op jit(solution)/shard_map/dot_general | solution.py:470
  94.4 2.8 %multiply_reduce_fusion.2 = (f32[128]{0:T(128)S(1)}, f32[128,768]{1,0:T(8,128)}, f32[128,768]{1,0:T(8,128)}) fusion(bf16[1,128,768]{2,1,0:T(8,128)(2,1)S(1)} %copy-done.5, f32[128,768]{1,0:T(8,128)} %convolution_add_fusion.5, bf16[768,768]{1,0:T(8,128)(2,1)} %bitcast.78, s32[]{:T(128)S(6)} %add.89, bf16[2048,768]{1,0:T(8,128)(2,1)S(1)} %bitcast.74), kind=kOutput, calls=%fused_computation.39 | convolution fusion | flops 151879552 | bytes 5702148 | tf_op jit(solution)/shard_map/dot_general | solution.py:470
  97.2 1.9 reshape.96
  99.3 1.4 multiply_reduce_fusion
  100.7 2.1 subtract_multiply_fusion
  102.8 1.8 reshape.97
  104.6 1.3 multiply_convert_fusion
  105.8 0.8 copy.13.cols_ref
  106.6 0.6 fusion.40
  107.2 54.4 %second.1 = (bf16[16,64,1536]{2,1,0:T(8,128)(2,1)}, bf16[16,48,128]{2,1,0:T(8,128)(2,1)}, bf16[16,768]{1,0:T(8,128)(2,1)}, bf16[16,768]{1,0:T(8,128)(2,1)}) custom-call(bf16[64,1536]{1,0:T(8,128)(2,1)} %get-tuple-element.39.mid_ref, bf16[768,128]{1,0:T(8,128)(2,1)} %copy.13.cols_ref, bf16[16,768]{1,0:T(8,128)(2,1)} %get-tuple-element.41.head_ref, ...), custom_call_target="tpu_custom_call" | custom-call | tf_op jit(solution)/shard_map/second/pallas_call | solution.py:337
  161.7 4.0 %fusion.1 = bf16[1,1024,288]{1,2,0:T(8,128)(2,1)} fusion(bf16[1024,1536]{1,0:T(8,128)(2,1)} %bitcast.100, bf16[1536,288]{0,1:T(8,128)(2,1)} %param.8), kind=kOutput, calls=%fused_computation.8 | convolution fusion | flops 906264576 | bytes 4620288 | tf_op jit(solution)/shard_map/dot_general | solution.py:470
  165.7 0.8 broadcast_select_fusion
  166.5 1.6 fusion.19
  168.5 0.9 copy-done.3
  169.8 0.9 copy-done.2
  172.1 0.9 fusion.21
  173.6 1.0 convolution_convert_fusion.2
  174.7 1.0 copy-done.15
  175.7 1.1 fusion
  176.9 0.7 pad.19.gain_ref
  178.0 56.5 %third.1 = (bf16[2,4,4,80,256]{4,3,2,1,0:T(8,128)(2,1)}, f32[24,128]{1,0:T(8,128)}) custom-call(bf16[2,4,4,80,256]{4,3,2,1,0:T(8,128)(2,1)} %bitcast.87, f32[24,128]{1,0:T(8,128)} %pad.19.gain_ref), custom_call_target="tpu_custom_call" | custom-call | tf_op jit(solution)/shard_map/third/pallas_call | solution.py:440
  234.5 1.1 fusion.39
  235.7 0.8 pad_maximum_fusion
  237.8 0.9 copy-done.13
  (63 shorter events, 4.7 us)
Async XLA Ops:
  79.2 5.5 %copy-start = (bf16[16,128,768]{2,1,0:T(8,128)(2,1)S(1)}, bf16[16,128,768]{2,1,0:T(8,128)(2,1)}, u32[]{:S(2)}) copy-start(bf16[16,128,768]{2,1,0:T(8,128)(2,1)} %get-tuple-element.15) | copy-start | bytes 9437188
  91.7 2.7 %copy-start.5 = (bf16[1,128,768]{2,1,0:T(8,128)(2,1)S(1)}, bf16[1,128,768]{2,1,0:T(8,128)(2,1)}, u32[]{:S(2)}) copy-start(bf16[1,128,768]{2,1,0:T(8,128)(2,1)} %param.6) | copy-start | bytes 589828
  94.4 4.9 %copy-start.12 = (f32[1536]{0:T(1024)S(1)}, f32[1536]{0:T(1024)}, u32[]{:S(2)}) copy-start(f32[1536]{0:T(1024)} %param.10) | copy-start | bytes 18436
  165.7 2.4 %copy-start.4 = (bf16[16,48,768]{2,1,0:T(8,128)(2,1)S(1)}, bf16[16,48,768]{2,1,0:T(8,128)(2,1)}, u32[]{:S(2)}) copy-start(bf16[16,48,768]{2,1,0:T(8,128)(2,1)} %get-tuple-element.33) | copy-start | bytes 3538948
  168.2 1.3 copy-start.3
  169.4 1.3 copy-start.2
  169.8 1.4 copy-start.1
  169.8 1.4 copy-start.11
  171.1 1.0 copy-start.6
  171.1 1.9 copy-start.9
  173.6 1.1 copy-start.10
  173.6 2.1 copy-start.15
  176.9 1.1 copy-start.7
  234.5 1.9 copy-start.14
  234.5 3.1 %copy-start.8 = (bf16[2,4,4,80,256]{4,3,2,1,0:T(8,128)(2,1)S(1)}, bf16[2,4,4,80,256]{4,3,2,1,0:T(8,128)(2,1)}, u32[]{:S(2)}) copy-start(bf16[2,4,4,80,256]{4,3,2,1,0:T(8,128)(2,1)} %get-tuple-element.22) | copy-start | bytes 3932164
  237.7 0.9 copy-start.13

commit v2 on v0

v2 whole, which is shorter than its diff:
```python
import functools
import math

import jax
import jax.numpy as jnp
from jax import lax
from jax.experimental import pallas as pl
from jax.experimental.pallas import tpu as pltpu
from jax.sharding import PartitionSpec as P

EPS = 1e-06
MESH = pl.DeviceIdType.MESH
F32 = jnp.float32
BF16 = jnp.bfloat16


def wrap4(i):
    return lax.rem(i + 8, 4)


class Place:
    def __init__(self):
        self.dp = lax.axis_index("dp")
        self.seq = lax.axis_index("seq")
        self.z_hi = self.dp // 8
        self.x = lax.rem(self.dp // 2, 4)
        self.core = lax.rem(self.dp, 2)
        self.y = self.seq // 4
        self.z = lax.rem(self.seq, 4)

    def at_seq(self, y, z):
        return (self.dp, y * 4 + z)

    def y_peer(self, step):
        return self.at_seq(wrap4(self.y + step), self.z)

    def z_peer(self, step):
        return self.at_seq(self.y, wrap4(self.z + step))

    def x_peer(self, step):
        return (self.z_hi * 8 + wrap4(self.x + step) * 2 + self.core, self.seq)

    def z_hi_peer(self, step):
        return (wrap4(self.z_hi + step) * 8 + self.x * 2 + self.core, self.seq)

    def other_core(self):
        return (self.z_hi * 8 + self.x * 2 + 1 - self.core, self.seq)


class Wire:
    def __init__(self, send_sems, recv_sems, anyone):
        self.send_sems = send_sems
        self.recv_sems = recv_sems
        self.anyone = anyone
        self.started = []
        self.names = {}

    def number(self, name):
        return self.names.setdefault(name, len(self.names))

    def send(self, name, src, dst, device):
        k = self.number(name)
        copy = pltpu.make_async_remote_copy(
            src_ref=src,
            dst_ref=dst,
            send_sem=self.send_sems.at[k],
            recv_sem=self.recv_sems.at[k],
            device_id=device,
            device_id_type=MESH,
        )
        copy.start()
        self.started.append(copy)

    def recv(self, name, ref):
        k = self.number(name)
        pltpu.make_async_remote_copy(
            src_ref=ref,
            dst_ref=ref,
            send_sem=self.send_sems.at[k],
            recv_sem=self.recv_sems.at[k],
            device_id=self.anyone,
            device_id_type=MESH,
        ).wait_recv()

    def drain(self):
        for copy in self.started:
            copy.wait_send()


class Gather:
    order = (0, 1, 3, 2)

    def __init__(self, wire, place, tag, view):
        self.wire, self.place, self.tag, self.view = wire, place, tag, view

    def block(self, step, d):
        p = self.place
        return self.view(wrap4(p.y + step) * 4 + wrap4(p.z - d))

    def round_ring(self, d, src):
        for step in (1, -1):
            self.wire.send((self.tag, "y", step, d), src, self.block(0, d), self.place.y_peer(step))

    def start(self, src):
        for d in (1, 3, 2):
            self.wire.send((self.tag, "z", d), src, self.block(0, 0), self.place.z_peer(d))
        self.round_ring(0, src)

    def own(self, d):
        got = self.block(0, d)
        self.wire.recv((self.tag, "z", d), got)
        self.round_ring(d, got)

    def near(self, d):
        for step in (1, -1):
            got = self.block(-step, d)
            self.wire.recv((self.tag, "y", step, d), got)
            if (step == 1) == (d in (0, 1)):
                self.wire.send((self.tag, "relay", d), got, got, self.place.y_peer(step))

    def far(self, d):
        self.wire.recv((self.tag, "relay", d), self.block(2, d))


class Reduce:
    ways = (1, 3, 2)

    def __init__(self, wire, place, tag, rows, scale, packed, core_recv, core_sum, x_recv, x_sum, z_recv, out):
        self.wire, self.place, self.tag, self.rows, self.scale = wire, place, tag, rows, scale
        self.packed, self.core_recv, self.core_sum = packed, core_recv, core_sum
        self.x_recv, self.x_sum, self.z_recv, self.out = x_recv, x_sum, z_recv, out

    def span(self, blocks, count):
        return pl.ds(pl.multiple_of(blocks * self.rows, 16), count * self.rows)

    def core(self):
        p = self.place
        self.wire.send((self.tag, "core"), self.packed.at[self.span((1 - p.core) * 16, 16)], self.core_recv, p.other_core())

    def x(self):
        p = self.place
        self.wire.recv((self.tag, "core"), self.core_recv)

        def add(x):
            mine = self.packed[self.span(p.core * 16 + x * 4, 4), :].astype(F32)
            here = self.span(x * 4, 4)
            self.core_sum[here, :] = (mine + self.core_recv[here, :].astype(F32)).astype(BF16)

        for d in self.ways:
            to = wrap4(p.x + d)
            add(to)
            self.wire.send((self.tag, "x", d), self.core_sum.at[self.span(to * 4, 4)], self.x_recv.at[d - 1], p.x_peer(d))
        add(p.x)

    def z(self):
        p = self.place
        for d in self.ways:
            self.wire.recv((self.tag, "x", d), self.x_recv.at[d - 1])

        def add(z):
            total = self.core_sum[self.span(p.x * 4 + z, 1), :].astype(F32)
            here = self.span(z, 1)
            for d in self.ways:
                total = total + self.x_recv[d - 1, here, :].astype(F32)
            self.x_sum[here, :] = total.astype(BF16)

        for d in (2, 1, 3):
            to = wrap4(p.z_hi + d)
            add(to)
            self.wire.send((self.tag, "z", d), self.x_sum.at[self.span(to, 1)], self.z_recv.at[d - 1], p.z_hi_peer(d))
        add(p.z_hi)

    def zz(self):
        p = self.place
        total = self.x_sum[self.span(p.z_hi, 1), :].astype(F32)
        for d in self.ways:
            self.wire.recv((self.tag, "z", d), self.z_recv.at[d - 1])
            total = total + self.z_recv[d - 1].astype(F32)
        here = self.span(p.core * 16 + p.x * 4 + p.z_hi, 1)
        self.out[here, :] = (total * self.scale).astype(BF16)
        mine = self.out.at[here]
        for d in (2, 1, 3):
            self.wire.send((self.tag, "zz", d), mine, mine, p.z_hi_peer(d))

    def xx(self):
        p = self.place
        for d in self.ways:
            self.wire.recv((self.tag, "zz", d), self.out.at[self.span(p.core * 16 + p.x * 4 + wrap4(p.z_hi - d), 1)])
        mine = self.out.at[self.span(p.core * 16 + p.x * 4, 4)]
        for d in self.ways:
            self.wire.send((self.tag, "xx", d), mine, mine, p.x_peer(d))

    def cc(self):
        p = self.place
        for d in self.ways:
            self.wire.recv((self.tag, "xx", d), self.out.at[self.span(p.core * 16 + wrap4(p.x - d) * 4, 4)])
        mine = self.out.at[self.span(p.core * 16, 16)]
        self.wire.send((self.tag, "cc"), mine, mine, p.other_core())

    def end(self):
        self.wire.recv((self.tag, "cc"), self.out.at[self.span((1 - self.place.core) * 16, 16)])


class GainSum:
    ways = (1, 3, 2)

    def __init__(self, wire, place, core_recv, held, got):
        self.wire, self.core_recv, self.held, self.got = wire, core_recv, held, got
        self.place = place
        self.peers = (place.x_peer, place.z_hi_peer, place.z_peer, place.y_peer)

    def start(self, src):
        self.wire.send("gain", src, self.core_recv, self.place.other_core())

    def spread(self, stage):
        for d in self.ways:
            self.wire.send(("gain", stage, d), self.held.at[stage], self.got.at[stage, d - 1], self.peers[stage](d))

    def total(self, stage):
        value = self.held[stage]
        for d in self.ways:
            self.wire.recv(("gain", stage, d), self.got.at[stage, d - 1])
            value = value + self.got[stage, d - 1]
        return value

    def first(self, src):
        self.wire.recv("gain", self.core_recv)
        self.held[0] = src[...] + self.core_recv[...]
        self.spread(0)

    def onward(self, stage):
        self.held[stage] = self.total(stage - 1)
        self.spread(stage)


def contract(a, b, dims):
    return lax.dot_general(a, b, (dims, ((), ())), preferred_element_type=F32)


def whole_kernel(
    scale, own, x_ref, taps_ref, wt_ref, cot_ref, gain_in_ref, gain_mid_ref,
    qkv_ref, input_grad_ref, kernel_ref, proj_ref, gains_ref,
    all_rows, all_taps, all_mid, all_cols,
    ext, ext_back, halo, shifted, conv, section, atwo, rtwo, section_grad, normed_grad, cols, cols_wide, cols_shifted,
    part, sums, far_send, far_recv, near_send, near_recv, column_send, z_recv,
    pacc,
    k_packed, k_core, k_csum, k_x, k_xsum, k_z, k_out,
    p_packed, p_core, p_csum, p_x, p_xsum, p_z, p_out,
    g_own, g_core, g_held, g_got,
    send_sems, recv_sems, local_sem,
):
    p = Place()
    wire = Wire(send_sems, recv_sems, p.other_core())
    length, chans = x_ref.shape
    half = length // 2
    width = 2 * chans
    shards = all_rows.shape[0]
    nlast = shards - 1

    def seq_peer(d):
        return (p.dp, lax.rem(p.seq + d, shards))

    peers = [seq_peer(d) for d in range(1, shards)]
    peers += [p.x_peer(d) for d in (1, 2, 3)] + [p.z_hi_peer(d) for d in (1, 2, 3)] + [p.other_core()]
    barrier = pltpu.get_barrier_semaphore()
    for peer in peers:
        pl.semaphore_signal(barrier, inc=1, device_id=peer, device_id_type=MESH)

    step_rows = 32

    def chunks(body, count=length, size=step_rows):
        @pl.loop(0, count // size)
        def _(i):
            body(pl.multiple_of(i * size, size))

    def first_norm(at, size=step_rows):
        x = x_ref[pl.ds(at, size), :].astype(F32)
        r = lax.rsqrt(jnp.mean(x * x, axis=-1, keepdims=True) + EPS)
        return x, r, x * r

    def norm_rows(at):
        normed = (first_norm(at)[2] * gain_in_ref[...]).astype(BF16)
        all_rows[p.seq, pl.ds(at, step_rows), :] = normed
        ext[pl.ds(8 + at, step_rows), :] = normed.astype(F32)

    chunks(norm_rows)
    pl.semaphore_wait(barrier, len(peers))

    lanes_half = chans // 2
    quarter = taps_ref.shape[0] // 4

    def core_lanes(core):
        return pl.ds(pl.multiple_of(core * lanes_half, 128), lanes_half)

    def piece(x):
        return pl.ds(pl.multiple_of(x * quarter, 16), quarter)

    my_lanes = core_lanes(p.core)
    own_taps = taps_ref.at[piece(p.x), my_lanes]
    taps = Gather(wire, p, "taps", lambda block: all_taps.at[block, piece(p.x), my_lanes])
    rows = Gather(wire, p, "rows", lambda block: all_rows.at[block])
    mid = Gather(wire, p, "mid", lambda block: all_mid.at[block])
    taps.start(own_taps)
    local = pltpu.make_async_copy(own_taps, all_taps.at[p.seq, piece(p.x), my_lanes], local_sem.at[0])
    local.start()
    wire.send("tail", ext.at[pl.ds(length, 8)], halo.at[0], seq_peer(1))
    wire.send("head", ext.at[pl.ds(8, 8)], halo.at[1], seq_peer(nlast))

    def x_part(x, column):
        return all_taps.at[pl.ds(wrap4(p.y + column) * 4, 4), piece(x), my_lanes]

    def x_send(column):
        mine = x_part(p.x, column)
        for way in (1, -1):
            wire.send(("x", way, column), mine, mine, p.x_peer(way))

    def x_relay(column):
        for way in (1, -1):
            got = x_part(wrap4(p.x - way), column)
            wire.recv(("x", way, column), got)
            if (way == 1) == (column in (0, 1)):
                wire.send(("xx", column), got, got, p.x_peer(way))

    def core_part(core, column):
        return all_taps.at[pl.ds(wrap4(p.y + column) * 4, 4), :, core_lanes(core)]

    def core_send(column):
        wire.recv(("xx", column), x_part(wrap4(p.x + 2), column))
        mine = core_part(p.core, column)
        wire.send(("core", column), mine, mine, p.other_core())

    span_rows = cot_ref.shape[1] // 4
    span_half = span_rows // 2
    tile = 256
    slot_of = {2: 0, 1: 1, -1: 2, 0: 3}

    def column_lanes(step):
        return pl.ds(pl.multiple_of(wrap4(p.y + step) * span_rows, 128), span_rows)

    def half_lanes(h):
        return pl.ds(h * chans, chans)

    def product(step, h):
        if h == 0:
            part[...] = cot_ref[:, column_lanes(step)].T

        @pl.loop(0, chans // tile)
        def _(n):
            span = pl.ds(pl.multiple_of(h * chans + n * tile, tile), tile)
            sums[slot_of[step], :, span] = contract(part[...], wt_ref[:, span], ((1,), (0,)))

    def far_out(h):
        lanes = half_lanes(h)
        far_send[:, lanes] = sums[0, :, lanes].astype(BF16)
        wire.send(("far+", h), far_send.at[pl.ds(0, span_half), lanes], far_recv.at[0, :, lanes], p.y_peer(1))
        wire.send(("far-", h), far_send.at[pl.ds(span_half, span_half), lanes], far_recv.at[1, :, lanes], p.y_peer(-1))

    def near_out(h):
        lanes = half_lanes(h)
        wire.recv(("far+", h), far_recv.at[0, :, lanes])
        near_send[0, :span_half, lanes] = (sums[1, :span_half, lanes] + far_recv[0, :, lanes].astype(F32)).astype(BF16)
        near_send[0, span_half:, lanes] = sums[1, span_half:, lanes].astype(BF16)
        wire.send(("near+", h), near_send.at[0, :, lanes], near_recv.at[0, :, lanes], p.y_peer(1))
        wire.recv(("far-", h), far_recv.at[1, :, lanes])
        near_send[1, :span_half, lanes] = sums[2, :span_half, lanes].astype(BF16)
        near_send[1, span_half:, lanes] = (sums[2, span_half:, lanes] + far_recv[1, :, lanes].astype(F32)).astype(BF16)
        wire.send(("near-", h), near_send.at[1, :, lanes], near_recv.at[1, :, lanes], p.y_peer(-1))

    def mid_out(h):
        lanes = half_lanes(h)
        wire.recv(("near+", h), near_recv.at[0, :, lanes])
        wire.recv(("near-", h), near_recv.at[1, :, lanes])

        @pl.loop(0, 4)
        def _(i):
            at = pl.ds(pl.multiple_of(i * half, 16), half)
            total = sums[3, at, lanes] + near_recv[0, at, lanes].astype(F32) + near_recv[1, at, lanes].astype(F32)
            sums[3, at, lanes] = total
            column_send[i, :, lanes] = total.astype(BF16)

        for d in (1, 3, 2):
            wire.send(("mid", h, d), column_send.at[wrap4(p.z + d), :, lanes], z_recv.at[d - 1, :, lanes], p.z_peer(d))

    def mid_in(h):
        for d in (1, 3, 2):
            wire.recv(("mid", h, d), z_recv.at[d - 1, :, half_lanes(h)])

    product(2, 0)
    far_out(0)
    product(2, 1)
    far_out(1)
    local.wait()
    for d in (1, 3, 2):
        taps.own(d)
    x_send(0)
    product(1, 0)
    product(1, 1)
    for d in taps.order:
        taps.near(d)
    x_send(1)
    x_send(-1)
    product(-1, 0)
    product(-1, 1)
    near_out(0)
    near_out(1)
    for d in taps.order:
        taps.far(d)
    x_send(2)
    rows.start(all_rows.at[p.seq])
    product(0, 0)
    product(0, 1)
    x_relay(0)
    mid_out(0)
    for d in (1, 3, 2):
        rows.own(d)
    x_relay(1)
    core_send(0)
    x_relay(-1)
    core_send(1)
    x_relay(2)
    core_send(-1)
    mid_out(1)
    core_send(2)
    for column in (0, 1, -1, 2):
        wire.recv(("core", column), core_part(1 - p.core, column))

    def taps_of(k, group, lanes=slice(None)):
        block = all_taps[group * (shards // 2) : (group + 1) * (shards // 2), k * own : (k + 1) * own, lanes]
        return block.reshape(lanes_half, -1)

    def edges(into, recv):
        into[0:8, :] = jnp.where(p.seq > 0, recv[0], 0.0)
        into[length + 8 : length + 16, :] = jnp.where(p.seq < nlast, recv[1], 0.0)

    wire.recv("tail", halo.at[0])
    wire.recv("head", halo.at[1])
    edges(ext, halo)
    for k in range(5):
        shifted[k] = ext[6 + k : 6 + k + length, :].astype(BF16)
    for group in range(2):
        total = contract(shifted[0], taps_of(0, group), ((1,), (1,)))
        for k in range(1, 5):
            total = total + contract(shifted[k], taps_of(k, group), ((1,), (1,)))
        conv[:, group * lanes_half : (group + 1) * lanes_half] = total

    def section_rows(at):
        here = pl.ds(at, step_rows)
        c = conv[here, :]
        value = x_ref[here, :].astype(F32) + c * jax.nn.sigmoid(c)
        for j in range(chans // 128):
            section[j, here, :] = value[:, j * 128 : (j + 1) * 128]

    chunks(section_rows)
    pool_rows = 16

    def pool(i):
        at = i * pool_rows
        here = slice(at, at + pool_rows)
        even, odd = (
            jnp.concatenate(
                [section[j, pl.ds(2 * at + i, pool_rows, stride=2), :] for j in range(chans // 128)], axis=1
            )
            for i in range(2)
        )
        squares = jnp.sum(even * even, axis=-1, keepdims=True) + jnp.sum(odd * odd, axis=-1, keepdims=True)
        r = lax.rsqrt(squares / width + EPS)
        rtwo[here, :] = jnp.broadcast_to(r, (pool_rows, 128))
        for j, value in enumerate((even * r, odd * r)):
            lanes = slice(j * chans, (j + 1) * chans)
            atwo[here, lanes] = value
            all_mid[p.seq, here, lanes] = (value * gain_mid_ref[j : j + 1, :]).astype(BF16)

    for i in range(half // pool_rows):
        pool(i)
    mid.start(all_mid.at[p.seq])

    mid_in(0)
    mid_in(1)
    g_own[...] = jnp.zeros_like(g_own)

    def pool_back(i):
        at = i * pool_rows
        here = slice(at, at + pool_rows)
        r = rtwo[here, 0:1]
        grads, terms = [], 0.0
        for j in range(2):
            lanes = slice(j * chans, (j + 1) * chans)
            there = pl.ds(pl.multiple_of(p.z * half + at, 16), pool_rows)
            grad = sums[3, there, lanes]
            for d in range(3):
                grad = grad + z_recv[d, here, lanes].astype(F32)
            a = atwo[here, lanes]
            g_own[1 + j : 2 + j, :] += jnp.sum(grad * a, axis=0, keepdims=True)
            g = gain_mid_ref[j : j + 1, :] * grad
            terms = terms + jnp.sum(g * a, axis=-1, keepdims=True)
            grads.append((g, a))
        for j, (g, a) in enumerate(grads):
            value = r * (g - a * (terms / width))
            for n in range(chans // 128):
                section_grad[n, pl.ds(2 * at + j, pool_rows, stride=2), :] = value[:, n * 128 : (n + 1) * 128]

    def section_grad_rows(here):
        return jnp.concatenate([section_grad[n, here, :] for n in range(chans // 128)], axis=1)

    for i in range(half // pool_rows):
        pool_back(i)

    def conv_back(at):
        here = pl.ds(at, step_rows)
        c = conv[here, :]
        s = jax.nn.sigmoid(c)
        grad = section_grad_rows(here) * s * (1.0 + c * (1.0 - s))
        ext_back[pl.ds(8 + at, step_rows), :] = grad.astype(BF16).astype(F32)

    chunks(conv_back)
    wire.send("tail back", ext_back.at[pl.ds(length, 8)], halo.at[2], seq_peer(1))
    wire.send("head back", ext_back.at[pl.ds(8, 8)], halo.at[3], seq_peer(nlast))
    for j in range(chans // 128):
        lanes = slice(j * 128, (j + 1) * 128)
        cols[lanes, :] = ext_back[8 : 8 + length, lanes].T.astype(BF16)

    def owned(j):
        return cols.at[pl.ds(pl.multiple_of(j * own, 16), own)]

    for d in range(1, shards):
        wire.send(("cols", d), owned(lax.rem(p.seq + d, shards)), all_cols.at[p.seq], seq_peer(d))
    all_cols[p.seq] = cols[pl.ds(pl.multiple_of(p.seq * own, 16), own), :]
    mid.own(1)
    mid.own(3)
    for d in rows.order:
        rows.near(d)
    mid.own(2)

    wire.recv("tail back", halo.at[2])
    wire.recv("head back", halo.at[3])
    edges(ext_back, halo.at[pl.ds(2, 2)])
    for k in range(5):
        shifted[k] = ext_back[10 - k : 10 - k + length, :].astype(BF16)

    def through(n):
        lanes = slice(n * lanes_half, (n + 1) * lanes_half)
        total = None
        for k in range(5):
            for group in range(2):
                left = shifted[k, :, group * lanes_half : (group + 1) * lanes_half]
                term = contract(left, taps_of(k, group, lanes), ((1,), (0,)))
                total = term if total is None else total + term
        normed_grad[:, lanes] = total

    def project(step, last=False):
        block = all_mid[pl.ds(wrap4(p.y + step) * 4, 4)].reshape(span_rows, width)
        qkv_ref[:, column_lanes(step)] = contract(wt_ref[...], block, ((1,), (1,))).astype(BF16)
        left = cot_ref[:, column_lanes(step)]
        for n in range(width // tile):
            span = slice(n * tile, (n + 1) * tile)
            term = contract(left, all_mid[pl.ds(wrap4(p.y + step) * 4, 4), :, span].reshape(span_rows, tile), ((1,), (0,)))
            if step != 0:
                term = term + pacc[:, span]
            if last:
                high = term.shape[0]
                for j in range(tile // 128):
                    at = (n * (tile // 128) + j) * high
                    p_packed[at : at + high, :] = term[:, j * 128 : (j + 1) * 128].astype(BF16)
            else:
                pacc[:, span] = term

    through(0)
    mid.near(0)
    mid.near(1)
    through(1)
    mid.near(3)
    mid.near(2)

    def last_rows(at):
        here = pl.ds(at, step_rows)
        _, r, a = first_norm(at)
        grad = normed_grad[here, :]
        h = gain_in_ref[...] * grad
        g_own[0:1, :] += jnp.sum(grad * a, axis=0, keepdims=True)
        mean = jnp.mean(h * a, axis=-1, keepdims=True)
        input_grad_ref[here, :] = (section_grad_rows(here) + r * (h - a * mean)).astype(BF16)

    chunks(last_rows)
    gains = GainSum(wire, p, g_core, g_held, g_got)
    gains.start(g_own)

    for d in rows.order:
        rows.far(d)
    for d in range(1, shards):
        wire.recv(("cols", d), all_cols.at[lax.rem(p.seq + shards - d, shards)])
    for j in range(shards):
        cols_wide[:, j * length : (j + 1) * length] = all_cols[j].astype(F32)
    total_rows = shards * length
    place = lax.broadcasted_iota(jnp.int32, (own, total_rows), 1)
    for k in range(5):
        turned = cols_wide[...] if k == 2 else pltpu.roll(cols_wide[...], (k - 2) % total_rows, 1)
        source = place + (2 - k)
        turned = jnp.where((source >= 0) & (source < total_rows), turned, 0.0)
        cols_shifted[k * own : (k + 1) * own, :] = turned.astype(BF16)
    high = 5 * own
    for n in range(chans // tile):
        right = all_rows[:, :, n * tile : (n + 1) * tile].reshape(total_rows, tile)
        term = contract(cols_shifted[...], right, ((1,), (0,)))
        for j in range(tile // 128):
            at = (n * (tile // 128) + j) * high
            k_packed[at : at + high, :] = term[:, j * 128 : (j + 1) * 128].astype(BF16)

    def zero_rest(packed, used):
        packed[used:, :] = jnp.zeros((packed.shape[0] - used, 128), BF16)

    zero_rest(k_packed, high * (chans // 128))
    zero_rest(p_packed, wt_ref.shape[0] * (width // 128))
    kernel_sum = Reduce(wire, p, "k", k_z.shape[1], scale, k_packed, k_core, k_csum, k_x, k_xsum, k_z, k_out)
    proj_sum = Reduce(wire, p, "p", p_z.shape[1], scale, p_packed, p_core, p_csum, p_x, p_xsum, p_z, p_out)
    kernel_sum.core()
    gains.first(g_own)
    project(0)
    kernel_sum.x()
    project(1)
    gains.onward(1)
    kernel_sum.z()
    project(-1)
    for d in mid.order:
        mid.far(d)
    project(2, last=True)
    proj_sum.core()
    kernel_sum.zz()
    gains.onward(2)
    proj_sum.x()
    kernel_sum.xx()
    gains.onward(3)
    proj_sum.z()
    kernel_sum.cc()
    gains_ref[...] = gains.total(3) * scale
    proj_sum.zz()
    kernel_sum.end()
    for j in range(chans // 128):
        kernel_ref[:, j * 128 : (j + 1) * 128] = k_out[j * high : (j + 1) * high, :]
    proj_sum.xx()
    proj_sum.cc()
    proj_sum.end()
    high = wt_ref.shape[0]
    for j in range(width // 128):
        proj_ref[:, j * 128 : (j + 1) * 128] = p_out[j * high : (j + 1) * high, :]
    wire.drain()


def reduce_scratch(elements):
    rows = -(-elements // (128 * 32 * 16)) * 16
    shapes = ((32 * rows, 128), (16 * rows, 128), (16 * rows, 128), (3, 4 * rows, 128), (4 * rows, 128), (3, rows, 128), (32 * rows, 128))
    return [pltpu.VMEM(shape, BF16) for shape in shapes]


def body(section_input, conv_kernel, qkv_weight, gain_in, gain_mid, qkv_cotangent):
    x = section_input[0]
    length, chans = x.shape
    half = length // 2
    width = 2 * chans
    shards = lax.axis_size("seq")
    own = conv_kernel.shape[2]
    high = qkv_weight.shape[1]
    scale = 1.0 / math.sqrt(lax.axis_size("dp") * shards * half)
    taps = jnp.transpose(conv_kernel, (0, 2, 1)).reshape(5 * own, chans)
    taps = jnp.pad(taps, ((0, -(5 * own) % 64), (0, 0)))
    positions = shards * half
    column = positions // 4
    total = shards * length
    vmem = pl.BlockSpec(memory_space=pltpu.VMEM)
    gain_shape = (8, chans)
    copies = 144
    qkv, input_grad, kernel, proj, gains = pl.pallas_call(
        functools.partial(whole_kernel, scale, own),
        name="whole",
        out_shape=(
            jax.ShapeDtypeStruct((high, positions), BF16),
            jax.ShapeDtypeStruct((length, chans), BF16),
            jax.ShapeDtypeStruct((5 * own, chans), BF16),
            jax.ShapeDtypeStruct((high, width), BF16),
            jax.ShapeDtypeStruct(gain_shape, F32),
        ),
        in_specs=[vmem] * 6,
        out_specs=(vmem,) * 5,
        scratch_shapes=[
            pltpu.VMEM((shards, length, chans), BF16),
            pltpu.VMEM((shards,) + taps.shape, BF16),
            pltpu.VMEM((shards, half, width), BF16),
            pltpu.VMEM((shards, own, length), BF16),
            pltpu.VMEM((length + 16, chans), F32),
            pltpu.VMEM((length + 16, chans), F32),
            pltpu.VMEM((4, 8, chans), F32),
            pltpu.VMEM((5, length, chans), BF16),
            pltpu.VMEM((length, chans), F32),
            pltpu.VMEM((chans // 128, length, 128), F32),
            pltpu.VMEM((half, width), F32),
            pltpu.VMEM((half, 128), F32),
            pltpu.VMEM((chans // 128, length, 128), F32),
            pltpu.VMEM((length, chans), F32),
            pltpu.VMEM((chans, length), BF16),
            pltpu.VMEM((own, total), F32),
            pltpu.VMEM((5 * own, total), BF16),
            pltpu.VMEM((column, high), BF16),
            pltpu.VMEM((4, column, width), F32),
            pltpu.VMEM((column, width), BF16),
            pltpu.VMEM((2, column // 2, width), BF16),
            pltpu.VMEM((2, column, width), BF16),
            pltpu.VMEM((2, column, width), BF16),
            pltpu.VMEM((4, half, width), BF16),
            pltpu.VMEM((3, half, width), BF16),
            pltpu.VMEM((high, width), F32),
            *reduce_scratch(5 * own * chans),
            *reduce_scratch(high * width),
            pltpu.VMEM(gain_shape, F32),
            pltpu.VMEM(gain_shape, F32),
            pltpu.VMEM((4,) + gain_shape, F32),
            pltpu.VMEM((4, 3) + gain_shape, F32),
            pltpu.SemaphoreType.DMA((copies,)),
            pltpu.SemaphoreType.DMA((copies,)),
            pltpu.SemaphoreType.DMA((1,)),
        ],
        compiler_params=pltpu.CompilerParams(collective_id=0, has_side_effects=True, vmem_limit_bytes=60 << 20),
    )(x, taps, qkv_weight.T, qkv_cotangent[0].T, gain_in[None], gain_mid.reshape(2, chans))
    return (
        qkv.T[None],
        input_grad[None],
        jnp.transpose(kernel.reshape(5, own, chans), (0, 2, 1)),
        gains[0],
        gains[1:3].reshape(width),
        proj.T,
    )


def solution(mesh):
    placed = (
        P("dp", "seq", None),
        P(None, None, "seq"),
        P(None, "seq"),
        P(),
        P(),
        P("dp", None, "seq"),
    )
    return jax.shard_map(
        body,
        mesh=mesh,
        in_specs=placed,
        out_specs=(
            P("dp", None, "seq"),
            P("dp", "seq", None),
            P(None, None, "seq"),
            P(),
            P(),
            P(None, "seq"),
        ),
        check_vma=False,
    )
```

time: 829 us -> 174 us (0.21)
  waiting for transfers between devices: 642 us -> 0 us
  Pallas kernels: 0 us -> 161 us
  blocking collectives: 113 us -> 0 us
  matrix products: 33.7 us -> 0 us
  between operations: 14 us -> 0.66 us
  other arithmetic: 12.6 us -> 0 us
  starting transfers between devices: 9.49 us -> 0 us
  local copies, waits for them, and re-layouts: 1.83 us -> 11 us
    all_gather x3 -> x0, waiting for transfers between devices: 314 us -> none  [the longest x1 150 us: body(): full_kernel = lax.all_gather(conv_kernel, 'seq', axis=2, tiled=True)]
    psum x1 -> x0, waiting for transfers between devices: 241 us -> none  [body(): kernel_total, proj_total = lax.psum((kernel_term, proj_grad), 'dp')]
    pallas_call x0 -> x1, Pallas kernels: none -> 161 us  [body(): pl.pallas_call(functools.partial(whole_kernel, scale, own), name='whole',...]
    psum x1 -> x0, blocking collectives: 113 us -> none  [body(): lax.psum((gain_in_term, gain_mid_term), ('dp', 'seq'))]
    reduce_scatter x1 -> x0, waiting for transfers between devices: 84 us -> none  [body(): lax.psum_scatter(lax.dot_general(grads_out, qkv_weight, (((1,), (1,)), ((...]
    dot_general x18 -> x0, matrix products: 33.7 us -> none  [the longest x5 8.12 us: backward_taps(): lax.dot_general(rows[4 - k:4 - k + length], kernel[k], (((1,), (1,)), (()...]
  transfers between devices with their start and end apart: 8 -> 0, of which waited for: 6 -> 0; matrix products, arithmetic and copies ran while one was open for 5% -> 0% of each run, Pallas kernels for 0% -> 0%
where the time goes in v2:
time: 174 us; the launch traced here: 173 us
  Pallas kernels  161 us (93%)
  local copies, waits for them, and re-layouts  11 us (6%)
    pallas_call x1, Pallas kernels, body(): pl.pallas_call(functools.partial(whole_kernel, scale, own), name='whole',...  161 us
    unnamed x12, local copies, waits for them, and re-layouts  4.72 us

profile of v2, /device:TPU:1, one launch (start us, length us, event | category | flops | bytes accessed | tf_op | source)
XLA Modules:
  0.0 173.2 jit_solution(3659741308457052651)
XLA Ops:
  0.6 0.0 copy-start.3
  0.6 1.3 broadcast_in_dim.9.gain_in_ref
  1.9 0.0 copy-done.3
  1.9 0.6 reshape.25.gain_mid_ref
  2.5 1.8 %pad.4.taps_ref = bf16[256,768]{1,0:T(8,128)(2,1)} pad(bf16[240,768]{1,0:T(8,128)(2,1)} %bitcast.20, bf16[]{:T(256)} %constant.2.clone.1), padding=0_16x0_0 | pad | bytes 761858 | tf_op jit(solution)/shard_map/jit(_pad)/pad | solution.py:664
  4.3 161.5 %whole.1 = (bf16[288,1024]{1,0:T(8,128)(2,1)}, bf16[128,768]{1,0:T(8,128)(2,1)}, bf16[240,768]{1,0:T(8,128)(2,1)}, bf16[288,1536]{1,0:T(8,128)(2,1)}, f32[8,768]{1,0:T(8,128)}) custom-call(bf16[128,768]{1,0:T(8,128)(2,1)} %bitcast.22, bf16[256,768]{1,0:T(8,128)(2,1)} %pad.4.taps_ref, bf16[288,1536]{1,0:T(8,128)(2,1)} %bitcast.16, ...), custom_call_target="tpu_custom_call" | custom-call | tf_op jit(solution)/shard_map/whole/pallas_call | solution.py:671
  165.8 1.3 slice_reduce_fusion
  167.1 0.7 slice.7
  167.8 0.6 reshape.27
  168.5 0.0 copy-start.2
  168.5 0.0 copy-start
  168.5 2.0 %copy.16 = bf16[1,1024,288]{1,2,0:T(8,128)(2,1)} copy(bf16[1,1024,288]{1,2,0:T(8,128)(2,1)} %bitcast.19) | data formatting | bytes 1179648
  170.5 0.0 copy-done.2
  170.5 0.0 copy-start.1
  170.5 0.7 copy.17
  171.1 0.4 copy-done.1
  171.5 0.7 copy.18
  172.3 0.0 copy-done
  172.3 0.9 copy.19
Async XLA Ops:
  0.6 1.3 copy-start.3
  168.5 2.0 %copy-start.2 = (bf16[128,768]{1,0:T(8,128)(2,1)S(1)}, bf16[128,768]{1,0:T(8,128)(2,1)}, u32[]{:S(2)}) copy-start(bf16[128,768]{1,0:T(8,128)(2,1)} %get-tuple-element.12) | copy-start | bytes 589828
  168.5 3.8 %copy-start = (bf16[288,1536]{1,0:T(8,128)(2,1)S(1)}, bf16[288,1536]{1,0:T(8,128)(2,1)}, u32[]{:S(2)}) copy-start(bf16[288,1536]{1,0:T(8,128)(2,1)} %get-tuple-element.15) | copy-start | bytes 2654212
  170.5 1.1 copy-start.1

commit v3 on v2

--- a/solution.py
+++ b/solution.py
@@ -137,14 +137,19 @@
         p = self.place
         self.wire.send((self.tag, "core"), self.packed.at[self.span((1 - p.core) * 16, 16)], self.core_recv, p.other_core())
 
+    def before_x(self):
+        self.wire.recv((self.tag, "core"), self.core_recv)
+
+    def chip_total(self, x):
+        mine = self.packed[self.span(self.place.core * 16 + x * 4, 4), :].astype(F32)
+        return mine + self.core_recv[self.span(x * 4, 4), :].astype(F32)
+
     def x(self):
         p = self.place
-        self.wire.recv((self.tag, "core"), self.core_recv)
+        self.before_x()
 
         def add(x):
-            mine = self.packed[self.span(p.core * 16 + x * 4, 4), :].astype(F32)
-            here = self.span(x * 4, 4)
-            self.core_sum[here, :] = (mine + self.core_recv[here, :].astype(F32)).astype(BF16)
+            self.core_sum[self.span(x * 4, 4), :] = self.chip_total(x).astype(BF16)
 
         for d in self.ways:
             to = wrap4(p.x + d)
@@ -201,6 +206,39 @@
         self.wire.recv((self.tag, "cc"), self.out.at[self.span((1 - self.place.core) * 16, 16)])
 
 
+class ReduceOverY(Reduce):
+    def core(self):
+        p = self.place
+        theirs = self.packed.at[:, self.span((1 - p.core) * 16, 16)]
+        self.wire.send((self.tag, "core"), theirs, self.core_recv, p.other_core())
+
+    def y(self, sums, got):
+        p = self.place
+        self.y_sums, self.y_got = sums, got
+        self.wire.recv((self.tag, "core"), self.core_recv)
+
+        def add(y):
+            mine = self.packed[y, self.span(p.core * 16, 16), :].astype(F32)
+            sums[y] = (mine + self.core_recv[y].astype(F32)).astype(BF16)
+
+        for d in self.ways:
+            to = wrap4(p.y + d)
+            add(to)
+            self.wire.send((self.tag, "y", d), sums.at[to], got.at[d - 1], p.y_peer(d))
+        add(p.y)
+
+    def before_x(self):
+        for d in self.ways:
+            self.wire.recv((self.tag, "y", d), self.y_got.at[d - 1])
+
+    def chip_total(self, x):
+        here = self.span(x * 4, 4)
+        total = self.y_sums[self.place.y, here, :].astype(F32)
+        for d in range(3):
+            total = total + self.y_got[d, here, :].astype(F32)
+        return total
+
+
 class GainSum:
     ways = (1, 3, 2)
 
@@ -240,11 +278,11 @@
 def whole_kernel(
     scale, own, x_ref, taps_ref, wt_ref, cot_ref, gain_in_ref, gain_mid_ref,
     qkv_ref, input_grad_ref, kernel_ref, proj_ref, gains_ref,
-    all_rows, all_taps, all_mid, all_cols,
-    ext, ext_back, halo, shifted, conv, section, atwo, rtwo, section_grad, normed_grad, cols, cols_wide, cols_shifted,
+    line_rows, line_shifted, all_taps, all_mid, all_cols, slab,
+    ext, ext_back, halo, shifted, conv, section, atwo, rtwo, section_grad, normed_grad, cols, cols_by_z,
     part, sums, far_send, far_recv, near_send, near_recv, column_send, z_recv,
     pacc,
-    k_packed, k_core, k_csum, k_x, k_xsum, k_z, k_out,
+    k_packed, k_core, k_csum, k_x, k_xsum, k_z, k_out, k_ysum, k_y,
     p_packed, p_core, p_csum, p_x, p_xsum, p_z, p_out,
     g_own, g_core, g_held, g_got,
     send_sems, recv_sems, local_sem,
@@ -254,14 +292,14 @@
     length, chans = x_ref.shape
     half = length // 2
     width = 2 * chans
-    shards = all_rows.shape[0]
+    shards = all_mid.shape[0]
     nlast = shards - 1
 
     def seq_peer(d):
         return (p.dp, lax.rem(p.seq + d, shards))
 
-    peers = [seq_peer(d) for d in range(1, shards)]
-    peers += [p.x_peer(d) for d in (1, 2, 3)] + [p.z_hi_peer(d) for d in (1, 2, 3)] + [p.other_core()]
+    peers = [seq_peer(1), seq_peer(nlast), p.other_core()]
+    peers += [peer(d) for peer in (p.x_peer, p.y_peer, p.z_peer, p.z_hi_peer) for d in (1, 2, 3)]
     barrier = pltpu.get_barrier_semaphore()
     for peer in peers:
         pl.semaphore_signal(barrier, inc=1, device_id=peer, device_id_type=MESH)
@@ -280,7 +318,6 @@
 
     def norm_rows(at):
         normed = (first_norm(at)[2] * gain_in_ref[...]).astype(BF16)
-        all_rows[p.seq, pl.ds(at, step_rows), :] = normed
         ext[pl.ds(8 + at, step_rows), :] = normed.astype(F32)
 
     chunks(norm_rows)
@@ -298,7 +335,6 @@
     my_lanes = core_lanes(p.core)
     own_taps = taps_ref.at[piece(p.x), my_lanes]
     taps = Gather(wire, p, "taps", lambda block: all_taps.at[block, piece(p.x), my_lanes])
-    rows = Gather(wire, p, "rows", lambda block: all_rows.at[block])
     mid = Gather(wire, p, "mid", lambda block: all_mid.at[block])
     taps.start(own_taps)
     local = pltpu.make_async_copy(own_taps, all_taps.at[p.seq, piece(p.x), my_lanes], local_sem.at[0])
@@ -342,12 +378,12 @@
 
     def product(step, h):
         if h == 0:
-            part[...] = cot_ref[:, column_lanes(step)].T
+            part[slot_of[step]] = cot_ref[:, column_lanes(step)].T
 
         @pl.loop(0, chans // tile)
         def _(n):
             span = pl.ds(pl.multiple_of(h * chans + n * tile, tile), tile)
-            sums[slot_of[step], :, span] = contract(part[...], wt_ref[:, span], ((1,), (0,)))
+            sums[slot_of[step], :, span] = contract(part[slot_of[step]], wt_ref[:, span], ((1,), (0,)))
 
     def far_out(h):
         lanes = half_lanes(h)
@@ -385,42 +421,51 @@
         for d in (1, 3, 2):
             wire.recv(("mid", h, d), z_recv.at[d - 1, :, half_lanes(h)])
 
+    def edges(into, recv):
+        into[0:8, :] = jnp.where(p.seq > 0, recv[0], 0.0)
+        into[length + 8 : length + 16, :] = jnp.where(p.seq < nlast, recv[1], 0.0)
+
     product(2, 0)
     far_out(0)
     product(2, 1)
-    far_out(1)
     local.wait()
     for d in (1, 3, 2):
         taps.own(d)
     x_send(0)
-    product(1, 0)
-    product(1, 1)
+    far_out(1)
+    wire.recv("tail", halo.at[0])
+    wire.recv("head", halo.at[1])
+    edges(ext, halo)
+    line_rows[p.z] = ext[...].astype(BF16)
+    for d in (1, 3, 2):
+        wire.send(("rows", d), line_rows.at[p.z], line_rows.at[p.z], p.z_peer(d))
     for d in taps.order:
         taps.near(d)
     x_send(1)
     x_send(-1)
+    product(1, 0)
     product(-1, 0)
-    product(-1, 1)
     near_out(0)
-    near_out(1)
     for d in taps.order:
         taps.far(d)
     x_send(2)
-    rows.start(all_rows.at[p.seq])
+    product(1, 1)
+    product(-1, 1)
+    near_out(1)
+    x_relay(0)
     product(0, 0)
     product(0, 1)
-    x_relay(0)
-    mid_out(0)
-    for d in (1, 3, 2):
-        rows.own(d)
     x_relay(1)
+    x_relay(-1)
     core_send(0)
-    x_relay(-1)
     core_send(1)
     x_relay(2)
+    mid_out(0)
     core_send(-1)
+    core_send(2)
     mid_out(1)
-    core_send(2)
+    for k in range(5):
+        shifted[k] = ext[6 + k : 6 + k + length, :].astype(BF16)
     for column in (0, 1, -1, 2):
         wire.recv(("core", column), core_part(1 - p.core, column))
 
@@ -428,15 +473,6 @@
         block = all_taps[group * (shards // 2) : (group + 1) * (shards // 2), k * own : (k + 1) * own, lanes]
         return block.reshape(lanes_half, -1)
 
-    def edges(into, recv):
-        into[0:8, :] = jnp.where(p.seq > 0, recv[0], 0.0)
-        into[length + 8 : length + 16, :] = jnp.where(p.seq < nlast, recv[1], 0.0)
-
-    wire.recv("tail", halo.at[0])
-    wire.recv("head", halo.at[1])
-    edges(ext, halo)
-    for k in range(5):
-        shifted[k] = ext[6 + k : 6 + k + length, :].astype(BF16)
     for group in range(2):
         total = contract(shifted[0], taps_of(0, group), ((1,), (1,)))
         for k in range(1, 5):
@@ -519,17 +555,15 @@
         lanes = slice(j * 128, (j + 1) * 128)
         cols[lanes, :] = ext_back[8 : 8 + length, lanes].T.astype(BF16)
 
-    def owned(j):
-        return cols.at[pl.ds(pl.multiple_of(j * own, 16), own)]
-
-    for d in range(1, shards):
-        wire.send(("cols", d), owned(lax.rem(p.seq + d, shards)), all_cols.at[p.seq], seq_peer(d))
-    all_cols[p.seq] = cols[pl.ds(pl.multiple_of(p.seq * own, 16), own), :]
+    for z in range(4):
+        for y in range(4):
+            block = 4 * y + z
+            cols_by_z[z, y * own : (y + 1) * own, :] = cols[block * own : (block + 1) * own, :]
+    for d in (1, 3, 2):
+        wire.send(("cols", d), cols_by_z.at[wrap4(p.z + d)], all_cols.at[p.z], p.z_peer(d))
+    all_cols[p.z] = cols_by_z[p.z]
     mid.own(1)
-    mid.own(3)
-    for d in rows.order:
-        rows.near(d)
-    mid.own(2)
+    mid.near(0)
 
     wire.recv("tail back", halo.at[2])
     wire.recv("head back", halo.at[3])
@@ -565,11 +599,9 @@
                 pacc[:, span] = term
 
     through(0)
-    mid.near(0)
+    mid.own(3)
     mid.near(1)
     through(1)
-    mid.near(3)
-    mid.near(2)
 
     def last_rows(at):
         here = pl.ds(at, step_rows)
@@ -584,60 +616,68 @@
     gains = GainSum(wire, p, g_core, g_held, g_got)
     gains.start(g_own)
 
-    for d in rows.order:
-        rows.far(d)
-    for d in range(1, shards):
-        wire.recv(("cols", d), all_cols.at[lax.rem(p.seq + shards - d, shards)])
-    for j in range(shards):
-        cols_wide[:, j * length : (j + 1) * length] = all_cols[j].astype(F32)
-    total_rows = shards * length
-    place = lax.broadcasted_iota(jnp.int32, (own, total_rows), 1)
+    mid.own(2)
+    mid.near(3)
+
+    for d in (1, 3, 2):
+        wire.recv(("rows", d), line_rows.at[wrap4(p.z - d)])
+
+    @pl.loop(0, 4)
+    def _(z):
+        slab[...] = line_rows[z].astype(F32)
+        for k in range(5):
+            at = pl.ds(pl.multiple_of(z * length, 128), length)
+            line_shifted[k, at, :] = slab[6 + k : 6 + k + length, :].astype(BF16)
+
+    for d in (1, 3, 2):
+        wire.recv(("cols", d), all_cols.at[wrap4(p.z - d)])
+    left = jnp.concatenate([all_cols[z] for z in range(4)], axis=1)
+    high = 5 * own
     for k in range(5):
-        turned = cols_wide[...] if k == 2 else pltpu.roll(cols_wide[...], (k - 2) % total_rows, 1)
-        source = place + (2 - k)
-        turned = jnp.where((source >= 0) & (source < total_rows), turned, 0.0)
-        cols_shifted[k * own : (k + 1) * own, :] = turned.astype(BF16)
-    high = 5 * own
-    for n in range(chans // tile):
-        right = all_rows[:, :, n * tile : (n + 1) * tile].reshape(total_rows, tile)
-        term = contract(cols_shifted[...], right, ((1,), (0,)))
-        for j in range(tile // 128):
-            at = (n * (tile // 128) + j) * high
-            k_packed[at : at + high, :] = term[:, j * 128 : (j + 1) * 128].astype(BF16)
+        for n in range(chans // tile):
+            term = contract(left, line_shifted[k, :, n * tile : (n + 1) * tile], ((1,), (0,)))
+            for j in range(tile // 128):
+                at = (n * (tile // 128) + j) * high + k * own
+                for y in range(4):
+                    value = term[y * own : (y + 1) * own, j * 128 : (j + 1) * 128]
+                    k_packed[y, at : at + own, :] = value.astype(BF16)
 
     def zero_rest(packed, used):
         packed[used:, :] = jnp.zeros((packed.shape[0] - used, 128), BF16)
 
-    zero_rest(k_packed, high * (chans // 128))
+    for y in range(4):
+        zero_rest(k_packed.at[y], high * (chans // 128))
     zero_rest(p_packed, wt_ref.shape[0] * (width // 128))
-    kernel_sum = Reduce(wire, p, "k", k_z.shape[1], scale, k_packed, k_core, k_csum, k_x, k_xsum, k_z, k_out)
+    kernel_sum = ReduceOverY(wire, p, "k", k_z.shape[1], scale, k_packed, k_core, k_csum, k_x, k_xsum, k_z, k_out)
     proj_sum = Reduce(wire, p, "p", p_z.shape[1], scale, p_packed, p_core, p_csum, p_x, p_xsum, p_z, p_out)
     kernel_sum.core()
+    mid.near(2)
     gains.first(g_own)
+    kernel_sum.y(k_ysum, k_y)
     project(0)
-    kernel_sum.x()
     project(1)
+    project(-1)
     gains.onward(1)
-    kernel_sum.z()
-    project(-1)
     for d in mid.order:
         mid.far(d)
     project(2, last=True)
     proj_sum.core()
-    kernel_sum.zz()
+    kernel_sum.x()
     gains.onward(2)
     proj_sum.x()
-    kernel_sum.xx()
+    kernel_sum.z()
     gains.onward(3)
     proj_sum.z()
-    kernel_sum.cc()
+    kernel_sum.zz()
     gains_ref[...] = gains.total(3) * scale
     proj_sum.zz()
+    kernel_sum.xx()
+    proj_sum.xx()
+    kernel_sum.cc()
+    proj_sum.cc()
     kernel_sum.end()
     for j in range(chans // 128):
         kernel_ref[:, j * 128 : (j + 1) * 128] = k_out[j * high : (j + 1) * high, :]
-    proj_sum.xx()
-    proj_sum.cc()
     proj_sum.end()
     high = wt_ref.shape[0]
     for j in range(width // 128):
@@ -645,9 +685,13 @@
     wire.drain()
 
 
-def reduce_scratch(elements):
+def reduce_scratch(elements, over_y=0):
     rows = -(-elements // (128 * 32 * 16)) * 16
-    shapes = ((32 * rows, 128), (16 * rows, 128), (16 * rows, 128), (3, 4 * rows, 128), (4 * rows, 128), (3, rows, 128), (32 * rows, 128))
+    lead = (over_y,) if over_y else ()
+    shapes = [lead + (32 * rows, 128), lead + (16 * rows, 128), (16 * rows, 128)]
+    shapes += [(3, 4 * rows, 128), (4 * rows, 128), (3, rows, 128), (32 * rows, 128)]
+    if over_y:
+        shapes += [(over_y, 16 * rows, 128), (over_y - 1, 16 * rows, 128)]
     return [pltpu.VMEM(shape, BF16) for shape in shapes]
 
 
@@ -664,7 +708,6 @@
     taps = jnp.pad(taps, ((0, -(5 * own) % 64), (0, 0)))
     positions = shards * half
     column = positions // 4
-    total = shards * length
     vmem = pl.BlockSpec(memory_space=pltpu.VMEM)
     gain_shape = (8, chans)
     copies = 144
@@ -681,10 +724,12 @@
         in_specs=[vmem] * 6,
         out_specs=(vmem,) * 5,
         scratch_shapes=[
-            pltpu.VMEM((shards, length, chans), BF16),
+            pltpu.VMEM((4, length + 16, chans), BF16),
+            pltpu.VMEM((5, 4 * length, chans), BF16),
             pltpu.VMEM((shards,) + taps.shape, BF16),
             pltpu.VMEM((shards, half, width), BF16),
-            pltpu.VMEM((shards, own, length), BF16),
+            pltpu.VMEM((4, 4 * own, length), BF16),
+            pltpu.VMEM((length + 16, chans), F32),
             pltpu.VMEM((length + 16, chans), F32),
             pltpu.VMEM((length + 16, chans), F32),
             pltpu.VMEM((4, 8, chans), F32),
@@ -696,9 +741,8 @@
             pltpu.VMEM((chans // 128, length, 128), F32),
             pltpu.VMEM((length, chans), F32),
             pltpu.VMEM((chans, length), BF16),
-            pltpu.VMEM((own, total), F32),
-            pltpu.VMEM((5 * own, total), BF16),
-            pltpu.VMEM((column, high), BF16),
+            pltpu.VMEM((4, 4 * own, length), BF16),
+            pltpu.VMEM((4, column, high), BF16),
             pltpu.VMEM((4, column, width), F32),
             pltpu.VMEM((column, width), BF16),
             pltpu.VMEM((2, column // 2, width), BF16),
@@ -707,7 +751,7 @@
             pltpu.VMEM((4, half, width), BF16),
             pltpu.VMEM((3, half, width), BF16),
             pltpu.VMEM((high, width), F32),
-            *reduce_scratch(5 * own * chans),
+            *reduce_scratch(5 * own * chans, 4),
             *reduce_scratch(high * width),
             pltpu.VMEM(gain_shape, F32),
             pltpu.VMEM(gain_shape, F32),

time: 174 us -> 163 us (0.937)
  the two profiles are of different devices: /device:TPU:1 before, /device:TPU:33 now
where the time goes in v3:
time: 163 us
  Pallas kernels  151 us (93%)
  local copies, waits for them, and re-layouts  11 us (7%)
    pallas_call x1, Pallas kernels, body(): pl.pallas_call(functools.partial(whole_kernel, scale, own), name='whole',...  151 us
    unnamed x12, local copies, waits for them, and re-layouts  4.72 us

profile of v3, /device:TPU:33, one launch (start us, length us, event | category | flops | bytes accessed | tf_op | source)
XLA Modules:
  0.0 162.6 jit_solution(15888499137180841718)
XLA Ops:
  0.6 0.0 copy-start.3
  0.6 1.3 broadcast_in_dim.9.gain_in_ref
  1.9 0.0 copy-done.3
  1.9 0.6 reshape.25.gain_mid_ref
  2.5 1.8 %pad.4.taps_ref = bf16[256,768]{1,0:T(8,128)(2,1)} pad(bf16[240,768]{1,0:T(8,128)(2,1)} %bitcast.20, bf16[]{:T(256)} %constant.2.clone.1), padding=0_16x0_0 | pad | bytes 761858 | tf_op jit(solution)/shard_map/jit(_pad)/pad | solution.py:708
  4.3 150.9 %whole.1 = (bf16[288,1024]{1,0:T(8,128)(2,1)}, bf16[128,768]{1,0:T(8,128)(2,1)}, bf16[240,768]{1,0:T(8,128)(2,1)}, bf16[288,1536]{1,0:T(8,128)(2,1)}, f32[8,768]{1,0:T(8,128)}) custom-call(bf16[128,768]{1,0:T(8,128)(2,1)} %bitcast.22, bf16[256,768]{1,0:T(8,128)(2,1)} %pad.4.taps_ref, bf16[288,1536]{1,0:T(8,128)(2,1)} %bitcast.16, ...), custom_call_target="tpu_custom_call" | custom-call | tf_op jit(solution)/shard_map/whole/pallas_call | solution.py:714
  155.2 1.3 slice_reduce_fusion
  156.5 0.7 slice.7
  157.2 0.6 reshape.27
  157.9 0.0 copy-start.2
  157.9 0.0 copy-start
  157.9 2.0 %copy.16 = bf16[1,1024,288]{1,2,0:T(8,128)(2,1)} copy(bf16[1,1024,288]{1,2,0:T(8,128)(2,1)} %bitcast.19) | data formatting | bytes 1179648
  159.9 0.0 copy-done.2
  159.9 0.0 copy-start.1
  159.9 0.7 copy.17
  160.5 0.4 copy-done.1
  160.9 0.7 copy.18
  161.7 0.0 copy-done
  161.7 0.9 copy.19
Async XLA Ops:
  0.6 1.3 copy-start.3
  157.9 2.0 %copy-start.2 = (bf16[128,768]{1,0:T(8,128)(2,1)S(1)}, bf16[128,768]{1,0:T(8,128)(2,1)}, u32[]{:S(2)}) copy-start(bf16[128,768]{1,0:T(8,128)(2,1)} %get-tuple-element.12) | copy-start | bytes 589828
  157.9 3.8 %copy-start = (bf16[288,1536]{1,0:T(8,128)(2,1)S(1)}, bf16[288,1536]{1,0:T(8,128)(2,1)}, u32[]{:S(2)}) copy-start(bf16[288,1536]{1,0:T(8,128)(2,1)} %get-tuple-element.15) | copy-start | bytes 2654212
  159.9 1.1 copy-start.1

commit v4 on v3

--- a/solution.py
+++ b/solution.py
@@ -186,24 +186,38 @@
         mine = self.out.at[here]
         for d in (2, 1, 3):
             self.wire.send((self.tag, "zz", d), mine, mine, p.z_hi_peer(d))
+        self.to_x(0)
+
+    def final(self, core, dx, dz, count=1):
+        p = self.place
+        z = wrap4(p.z_hi - dz) if count == 1 else 0
+        return self.out.at[self.span(core * 16 + wrap4(p.x - dx) * 4 + z, count)]
+
+    def to_x(self, dz):
+        p = self.place
+        mine = self.final(p.core, 0, dz)
+        for d in self.ways:
+            self.wire.send((self.tag, "xx", d, dz), mine, mine, p.x_peer(d))
+
+    def to_core(self, dx):
+        mine = self.final(self.place.core, dx, 0, 4)
+        self.wire.send((self.tag, "cc", dx), mine, mine, self.place.other_core())
 
     def xx(self):
-        p = self.place
-        for d in self.ways:
-            self.wire.recv((self.tag, "zz", d), self.out.at[self.span(p.core * 16 + p.x * 4 + wrap4(p.z_hi - d), 1)])
-        mine = self.out.at[self.span(p.core * 16 + p.x * 4, 4)]
-        for d in self.ways:
-            self.wire.send((self.tag, "xx", d), mine, mine, p.x_peer(d))
+        for dz in (1, 3, 2):
+            self.wire.recv((self.tag, "zz", dz), self.final(self.place.core, 0, dz))
+            self.to_x(dz)
+        self.to_core(0)
 
     def cc(self):
-        p = self.place
-        for d in self.ways:
-            self.wire.recv((self.tag, "xx", d), self.out.at[self.span(p.core * 16 + wrap4(p.x - d) * 4, 4)])
-        mine = self.out.at[self.span(p.core * 16, 16)]
-        self.wire.send((self.tag, "cc"), mine, mine, p.other_core())
+        for dx in self.ways:
+            for dz in (0, 1, 3, 2):
+                self.wire.recv((self.tag, "xx", dx, dz), self.final(self.place.core, dx, dz))
+            self.to_core(dx)
 
     def end(self):
-        self.wire.recv((self.tag, "cc"), self.out.at[self.span((1 - self.place.core) * 16, 16)])
+        for dx in (0, 1, 3, 2):
+            self.wire.recv((self.tag, "cc", dx), self.final(1 - self.place.core, dx, 0, 4))
 
 
 class ReduceOverY(Reduce):
@@ -276,8 +290,8 @@
 
 
 def whole_kernel(
-    scale, own, x_ref, taps_ref, wt_ref, cot_ref, gain_in_ref, gain_mid_ref,
-    qkv_ref, input_grad_ref, kernel_ref, proj_ref, gains_ref,
+    scale, own, x_ref, taps_ref, wt_ref, cot_ref, gain_ref,
+    qkv_ref, input_grad_ref, kernel_ref, proj_ref, gain_in_out, gain_mid_out,
     line_rows, line_shifted, all_taps, all_mid, all_cols, slab,
     ext, ext_back, halo, shifted, conv, section, atwo, rtwo, section_grad, normed_grad, cols, cols_by_z,
     part, sums, far_send, far_recv, near_send, near_recv, column_send, z_recv,
@@ -285,7 +299,7 @@
     k_packed, k_core, k_csum, k_x, k_xsum, k_z, k_out, k_ysum, k_y,
     p_packed, p_core, p_csum, p_x, p_xsum, p_z, p_out,
     g_own, g_core, g_held, g_got,
-    send_sems, recv_sems, local_sem,
+    send_sems, recv_sems,
 ):
     p = Place()
     wire = Wire(send_sems, recv_sems, p.other_core())
@@ -300,6 +314,9 @@
 
     peers = [seq_peer(1), seq_peer(nlast), p.other_core()]
     peers += [peer(d) for peer in (p.x_peer, p.y_peer, p.z_peer, p.z_hi_peer) for d in (1, 2, 3)]
+    own_rows, pad_rows = taps_ref.shape[0], all_taps.shape[1]
+    all_taps[p.seq, 0:own_rows, :] = taps_ref[...]
+    all_taps[p.seq, own_rows:pad_rows, :] = jnp.zeros((pad_rows - own_rows, chans), BF16)
     barrier = pltpu.get_barrier_semaphore()
     for peer in peers:
         pl.semaphore_signal(barrier, inc=1, device_id=peer, device_id_type=MESH)
@@ -317,28 +334,28 @@
         return x, r, x * r
 
     def norm_rows(at):
-        normed = (first_norm(at)[2] * gain_in_ref[...]).astype(BF16)
+        normed = (first_norm(at)[2] * gain_ref[0:1, :]).astype(BF16)
         ext[pl.ds(8 + at, step_rows), :] = normed.astype(F32)
 
     chunks(norm_rows)
     pl.semaphore_wait(barrier, len(peers))
 
     lanes_half = chans // 2
-    quarter = taps_ref.shape[0] // 4
+    whole_rows = pad_rows // 4
+    quarter = (pad_rows - whole_rows) // 4
 
     def core_lanes(core):
         return pl.ds(pl.multiple_of(core * lanes_half, 128), lanes_half)
 
     def piece(x):
-        return pl.ds(pl.multiple_of(x * quarter, 16), quarter)
+        return pl.ds(pl.multiple_of(whole_rows + x * quarter, 16), quarter)
 
     my_lanes = core_lanes(p.core)
-    own_taps = taps_ref.at[piece(p.x), my_lanes]
-    taps = Gather(wire, p, "taps", lambda block: all_taps.at[block, piece(p.x), my_lanes])
+    taps_part = Gather(wire, p, "part", lambda block: all_taps.at[block, piece(p.x), my_lanes])
+    taps_whole = Gather(wire, p, "whole", lambda block: all_taps.at[block, pl.ds(0, whole_rows), my_lanes])
     mid = Gather(wire, p, "mid", lambda block: all_mid.at[block])
-    taps.start(own_taps)
-    local = pltpu.make_async_copy(own_taps, all_taps.at[p.seq, piece(p.x), my_lanes], local_sem.at[0])
-    local.start()
+    for taps in (taps_part, taps_whole):
+        taps.start(taps.block(0, 0))
     wire.send("tail", ext.at[pl.ds(length, 8)], halo.at[0], seq_peer(1))
     wire.send("head", ext.at[pl.ds(8, 8)], halo.at[1], seq_peer(nlast))
 
@@ -428,10 +445,11 @@
     product(2, 0)
     far_out(0)
     product(2, 1)
-    local.wait()
     for d in (1, 3, 2):
-        taps.own(d)
+        taps_part.own(d)
     x_send(0)
+    for d in (1, 3, 2):
+        taps_whole.own(d)
     far_out(1)
     wire.recv("tail", halo.at[0])
     wire.recv("head", halo.at[1])
@@ -439,15 +457,17 @@
     line_rows[p.z] = ext[...].astype(BF16)
     for d in (1, 3, 2):
         wire.send(("rows", d), line_rows.at[p.z], line_rows.at[p.z], p.z_peer(d))
-    for d in taps.order:
-        taps.near(d)
+    for d in taps_part.order:
+        taps_part.near(d)
     x_send(1)
     x_send(-1)
+    for d in taps_whole.order:
+        taps_whole.near(d)
     product(1, 0)
     product(-1, 0)
     near_out(0)
-    for d in taps.order:
-        taps.far(d)
+    for d in taps_part.order:
+        taps_part.far(d)
     x_send(2)
     product(1, 1)
     product(-1, 1)
@@ -455,17 +475,18 @@
     x_relay(0)
     product(0, 0)
     product(0, 1)
+    for d in taps_whole.order:
+        taps_whole.far(d)
+    for k in range(5):
+        shifted[k] = ext[6 + k : 6 + k + length, :].astype(BF16)
     x_relay(1)
     x_relay(-1)
     core_send(0)
+    x_relay(2)
     core_send(1)
-    x_relay(2)
-    mid_out(0)
     core_send(-1)
     core_send(2)
-    mid_out(1)
-    for k in range(5):
-        shifted[k] = ext[6 + k : 6 + k + length, :].astype(BF16)
+    mid_out(0)
     for column in (0, 1, -1, 2):
         wire.recv(("core", column), core_part(1 - p.core, column))
 
@@ -504,11 +525,17 @@
         for j, value in enumerate((even * r, odd * r)):
             lanes = slice(j * chans, (j + 1) * chans)
             atwo[here, lanes] = value
-            all_mid[p.seq, here, lanes] = (value * gain_mid_ref[j : j + 1, :]).astype(BF16)
+            all_mid[p.seq, here, lanes] = (value * gain_ref[1 + j : 2 + j, :]).astype(BF16)
 
     for i in range(half // pool_rows):
         pool(i)
     mid.start(all_mid.at[p.seq])
+    mid.own(1)
+    mid_out(1)
+    mid.own(3)
+    mid.near(0)
+    mid.near(1)
+    mid.own(2)
 
     mid_in(0)
     mid_in(1)
@@ -527,7 +554,7 @@
                 grad = grad + z_recv[d, here, lanes].astype(F32)
             a = atwo[here, lanes]
             g_own[1 + j : 2 + j, :] += jnp.sum(grad * a, axis=0, keepdims=True)
-            g = gain_mid_ref[j : j + 1, :] * grad
+            g = gain_ref[1 + j : 2 + j, :] * grad
             terms = terms + jnp.sum(g * a, axis=-1, keepdims=True)
             grads.append((g, a))
         for j, (g, a) in enumerate(grads):
@@ -562,8 +589,7 @@
     for d in (1, 3, 2):
         wire.send(("cols", d), cols_by_z.at[wrap4(p.z + d)], all_cols.at[p.z], p.z_peer(d))
     all_cols[p.z] = cols_by_z[p.z]
-    mid.own(1)
-    mid.near(0)
+    mid.near(3)
 
     wire.recv("tail back", halo.at[2])
     wire.recv("head back", halo.at[3])
@@ -599,15 +625,14 @@
                 pacc[:, span] = term
 
     through(0)
-    mid.own(3)
-    mid.near(1)
+    mid.near(2)
     through(1)
 
     def last_rows(at):
         here = pl.ds(at, step_rows)
         _, r, a = first_norm(at)
         grad = normed_grad[here, :]
-        h = gain_in_ref[...] * grad
+        h = gain_ref[0:1, :] * grad
         g_own[0:1, :] += jnp.sum(grad * a, axis=0, keepdims=True)
         mean = jnp.mean(h * a, axis=-1, keepdims=True)
         input_grad_ref[here, :] = (section_grad_rows(here) + r * (h - a * mean)).astype(BF16)
@@ -615,9 +640,6 @@
     chunks(last_rows)
     gains = GainSum(wire, p, g_core, g_held, g_got)
     gains.start(g_own)
-
-    mid.own(2)
-    mid.near(3)
 
     for d in (1, 3, 2):
         wire.recv(("rows", d), line_rows.at[wrap4(p.z - d)])
@@ -651,7 +673,6 @@
     kernel_sum = ReduceOverY(wire, p, "k", k_z.shape[1], scale, k_packed, k_core, k_csum, k_x, k_xsum, k_z, k_out)
     proj_sum = Reduce(wire, p, "p", p_z.shape[1], scale, p_packed, p_core, p_csum, p_x, p_xsum, p_z, p_out)
     kernel_sum.core()
-    mid.near(2)
     gains.first(g_own)
     kernel_sum.y(k_ysum, k_y)
     project(0)
@@ -669,7 +690,9 @@
     gains.onward(3)
     proj_sum.z()
     kernel_sum.zz()
-    gains_ref[...] = gains.total(3) * scale
+    gain_total = gains.total(3) * scale
+    gain_in_out[...] = gain_total[0:1, :]
+    gain_mid_out[...] = gain_total[1:3, :]
     proj_sum.zz()
     kernel_sum.xx()
     proj_sum.xx()
@@ -705,13 +728,13 @@
     high = qkv_weight.shape[1]
     scale = 1.0 / math.sqrt(lax.axis_size("dp") * shards * half)
     taps = jnp.transpose(conv_kernel, (0, 2, 1)).reshape(5 * own, chans)
-    taps = jnp.pad(taps, ((0, -(5 * own) % 64), (0, 0)))
+    pad_rows = -(-5 * own // 256) * 256
     positions = shards * half
     column = positions // 4
     vmem = pl.BlockSpec(memory_space=pltpu.VMEM)
     gain_shape = (8, chans)
-    copies = 144
-    qkv, input_grad, kernel, proj, gains = pl.pallas_call(
+    copies = 160
+    qkv, input_grad, kernel, proj, gain_in_grad, gain_mid_grad = pl.pallas_call(
         functools.partial(whole_kernel, scale, own),
         name="whole",
         out_shape=(
@@ -719,14 +742,15 @@
             jax.ShapeDtypeStruct((length, chans), BF16),
             jax.ShapeDtypeStruct((5 * own, chans), BF16),
             jax.ShapeDtypeStruct((high, width), BF16),
-            jax.ShapeDtypeStruct(gain_shape, F32),
+            jax.ShapeDtypeStruct((1, chans), F32),
+            jax.ShapeDtypeStruct((2, chans), F32),
         ),
-        in_specs=[vmem] * 6,
-        out_specs=(vmem,) * 5,
+        in_specs=[vmem] * 5,
+        out_specs=(vmem,) * 6,
         scratch_shapes=[
             pltpu.VMEM((4, length + 16, chans), BF16),
             pltpu.VMEM((5, 4 * length, chans), BF16),
-            pltpu.VMEM((shards,) + taps.shape, BF16),
+            pltpu.VMEM((shards, pad_rows, chans), BF16),
             pltpu.VMEM((shards, half, width), BF16),
             pltpu.VMEM((4, 4 * own, length), BF16),
             pltpu.VMEM((length + 16, chans), F32),
@@ -759,16 +783,15 @@
             pltpu.VMEM((4, 3) + gain_shape, F32),
             pltpu.SemaphoreType.DMA((copies,)),
             pltpu.SemaphoreType.DMA((copies,)),
-            pltpu.SemaphoreType.DMA((1,)),
         ],
         compiler_params=pltpu.CompilerParams(collective_id=0, has_side_effects=True, vmem_limit_bytes=60 << 20),
-    )(x, taps, qkv_weight.T, qkv_cotangent[0].T, gain_in[None], gain_mid.reshape(2, chans))
+    )(x, taps, qkv_weight.T, qkv_cotangent[0].T, jnp.concatenate([gain_in, gain_mid]).reshape(3, chans))
     return (
         qkv.T[None],
         input_grad[None],
         jnp.transpose(kernel.reshape(5, own, chans), (0, 2, 1)),
-        gains[0],
-        gains[1:3].reshape(width),
+        gain_in_grad.reshape(chans),
+        gain_mid_grad.reshape(width),
         proj.T,
     )
 

time: 163 us -> 154 us (0.945)
  the two profiles are of different devices: /device:TPU:33 before, /device:TPU:1 now
where the time goes in v4:
time: 154 us; the launch traced here: 153 us
  Pallas kernels  144 us (94%)
  local copies, waits for them, and re-layouts  6.7 us (4%)
    pallas_call x1, Pallas kernels, body(): pl.pallas_call(functools.partial(whole_kernel, scale, own), name='whole',...  144 us
    unnamed x14, local copies, waits for them, and re-layouts  5.48 us

profile of v4, /device:TPU:1, one launch (start us, length us, event | category | flops | bytes accessed | tf_op | source)
XLA Modules:
  0.0 152.8 jit_solution(17371404226204225895)
XLA Ops:
  0.6 0.7 pad_maximum_fusion
  1.3 0.6 reshape.28.gain_ref
  2.0 144.1 %whole.1 = (bf16[288,1024]{1,0:T(8,128)(2,1)}, bf16[128,768]{1,0:T(8,128)(2,1)}, bf16[240,768]{1,0:T(8,128)(2,1)}, bf16[288,1536]{1,0:T(8,128)(2,1)}, f32[1,768]{1,0:T(1,128)}, /*index=5*/f32[2,768]{1,0:T(2,128)}) custom-call(bf16[128,768]{1,0:T(8,128)(2,1)} %bitcast.23, bf16[240,768]{1,0:T(8,128)(2,1)} %bitcast.20, bf16[288,1536]{1,0:T(8,128)(2,1)} %bitcast.17, ...), custom_call_target="tpu_custom_call" | custom-call | tf_op jit(solution)/shard_map/whole/pallas_call | solution.py:737
  146.1 0.0 copy-start.3
  146.1 0.7 copy-done.3
  146.8 0.0 copy-start.4
  146.8 0.6 reshape.31
  147.4 0.1 copy-done.4
  147.5 0.6 reduce
  148.1 0.0 copy-start.2
  148.1 0.0 copy-start
  148.1 2.0 %copy.16 = bf16[1,1024,288]{1,2,0:T(8,128)(2,1)} copy(bf16[1,1024,288]{1,2,0:T(8,128)(2,1)} %bitcast.18) | data formatting | bytes 1179648
  150.1 0.0 copy-done.2
  150.1 0.0 copy-start.1
  150.1 0.7 copy.17
  150.8 0.4 copy-done.1
  151.1 0.7 copy.18
  151.9 0.0 copy-done
  151.9 0.9 copy.19
Async XLA Ops:
  146.1 0.7 copy-start.3
  146.8 0.7 copy-start.4
  148.1 2.0 %copy-start.2 = (bf16[128,768]{1,0:T(8,128)(2,1)S(1)}, bf16[128,768]{1,0:T(8,128)(2,1)}, u32[]{:S(2)}) copy-start(bf16[128,768]{1,0:T(8,128)(2,1)} %get-tuple-element.13) | copy-start | bytes 589828
  148.1 3.8 %copy-start = (bf16[288,1536]{1,0:T(8,128)(2,1)S(1)}, bf16[288,1536]{1,0:T(8,128)(2,1)}, u32[]{:S(2)}) copy-start(bf16[288,1536]{1,0:T(8,128)(2,1)} %get-tuple-element.17) | copy-start | bytes 2654212
  150.1 1.1 copy-start.1

commit v5 on v4

--- a/solution.py
+++ b/solution.py
@@ -101,9 +101,12 @@
         for step in (1, -1):
             self.wire.send((self.tag, "y", step, d), src, self.block(0, d), self.place.y_peer(step))
 
+    def line(self, ds, src):
+        for d in ds:
+            self.wire.send((self.tag, "z", d), src, self.block(0, 0), self.place.z_peer(d))
+
     def start(self, src):
-        for d in (1, 3, 2):
-            self.wire.send((self.tag, "z", d), src, self.block(0, 0), self.place.z_peer(d))
+        self.line((1, 3, 2), src)
         self.round_ring(0, src)
 
     def own(self, d):
@@ -353,7 +356,11 @@
     my_lanes = core_lanes(p.core)
     taps_part = Gather(wire, p, "part", lambda block: all_taps.at[block, piece(p.x), my_lanes])
     taps_whole = Gather(wire, p, "whole", lambda block: all_taps.at[block, pl.ds(0, whole_rows), my_lanes])
-    mid = Gather(wire, p, "mid", lambda block: all_mid.at[block])
+    mid_rows = half // 2
+    mids = [
+        Gather(wire, p, ("mid", i), lambda block, i=i: all_mid.at[block, pl.ds(i * mid_rows, mid_rows)])
+        for i in range(2)
+    ]
     for taps in (taps_part, taps_whole):
         taps.start(taps.block(0, 0))
     wire.send("tail", ext.at[pl.ds(length, 8)], halo.at[0], seq_peer(1))
@@ -450,7 +457,6 @@
     x_send(0)
     for d in (1, 3, 2):
         taps_whole.own(d)
-    far_out(1)
     wire.recv("tail", halo.at[0])
     wire.recv("head", halo.at[1])
     edges(ext, halo)
@@ -466,12 +472,12 @@
     product(1, 0)
     product(-1, 0)
     near_out(0)
+    far_out(1)
     for d in taps_part.order:
         taps_part.far(d)
     x_send(2)
     product(1, 1)
     product(-1, 1)
-    near_out(1)
     x_relay(0)
     product(0, 0)
     product(0, 1)
@@ -481,12 +487,13 @@
         shifted[k] = ext[6 + k : 6 + k + length, :].astype(BF16)
     x_relay(1)
     x_relay(-1)
+    x_relay(2)
     core_send(0)
-    x_relay(2)
     core_send(1)
+    mid_out(0)
     core_send(-1)
     core_send(2)
-    mid_out(0)
+    near_out(1)
     for column in (0, 1, -1, 2):
         wire.recv(("core", column), core_part(1 - p.core, column))
 
@@ -529,13 +536,29 @@
 
     for i in range(half // pool_rows):
         pool(i)
-    mid.start(all_mid.at[p.seq])
-    mid.own(1)
+    for mid in mids:
+        mid.round_ring(0, mid.block(0, 0))
+        mid.line((1, 3), mid.block(0, 0))
     mid_out(1)
-    mid.own(3)
-    mid.near(0)
-    mid.near(1)
-    mid.own(2)
+    for mid in mids:
+        mid.line((2,), mid.block(0, 0))
+    for d in (1, 3, 2):
+        wire.recv(("rows", d), line_rows.at[wrap4(p.z - d)])
+
+    @pl.loop(0, 4)
+    def _(z):
+        slab[...] = line_rows[z].astype(F32)
+        for k in range(5):
+            at = pl.ds(pl.multiple_of(z * length, 128), length)
+            line_shifted[k, at, :] = slab[6 + k : 6 + k + length, :].astype(BF16)
+
+    for mid in mids:
+        mid.own(1)
+    for mid in mids:
+        mid.own(3)
+    for d in (0, 1, 3):
+        for mid in mids:
+            mid.near(d)
 
     mid_in(0)
     mid_in(1)
@@ -589,7 +612,7 @@
     for d in (1, 3, 2):
         wire.send(("cols", d), cols_by_z.at[wrap4(p.z + d)], all_cols.at[p.z], p.z_peer(d))
     all_cols[p.z] = cols_by_z[p.z]
-    mid.near(3)
+    mids[0].own(2)
 
     wire.recv("tail back", halo.at[2])
     wire.recv("head back", halo.at[3])
@@ -625,7 +648,7 @@
                 pacc[:, span] = term
 
     through(0)
-    mid.near(2)
+    mids[1].own(2)
     through(1)
 
     def last_rows(at):
@@ -641,15 +664,8 @@
     gains = GainSum(wire, p, g_core, g_held, g_got)
     gains.start(g_own)
 
-    for d in (1, 3, 2):
-        wire.recv(("rows", d), line_rows.at[wrap4(p.z - d)])
-
-    @pl.loop(0, 4)
-    def _(z):
-        slab[...] = line_rows[z].astype(F32)
-        for k in range(5):
-            at = pl.ds(pl.multiple_of(z * length, 128), length)
-            line_shifted[k, at, :] = slab[6 + k : 6 + k + length, :].astype(BF16)
+    for mid in mids:
+        mid.near(2)
 
     for d in (1, 3, 2):
         wire.recv(("cols", d), all_cols.at[wrap4(p.z - d)])
@@ -679,8 +695,9 @@
     project(1)
     project(-1)
     gains.onward(1)
-    for d in mid.order:
-        mid.far(d)
+    for mid in mids:
+        for d in mid.order:
+            mid.far(d)
     project(2, last=True)
     proj_sum.core()
     kernel_sum.x()
@@ -733,7 +750,7 @@
     column = positions // 4
     vmem = pl.BlockSpec(memory_space=pltpu.VMEM)
     gain_shape = (8, chans)
-    copies = 160
+    copies = 176
     qkv, input_grad, kernel, proj, gain_in_grad, gain_mid_grad = pl.pallas_call(
         functools.partial(whole_kernel, scale, own),
         name="whole",

time: 154 us -> 151 us (0.981)
  Pallas kernels: 144 us -> 140 us
    pallas_call x1, Pallas kernels: 144 us -> 140 us  [body(): pl.pallas_call(functools.partial(whole_kernel, scale, own), name='whole',...]
where the time goes in v5:
time: 151 us; the launch traced here: 149 us
  Pallas kernels  140 us (93%)
  local copies, waits for them, and re-layouts  6.7 us (4%)
    pallas_call x1, Pallas kernels, body(): pl.pallas_call(functools.partial(whole_kernel, scale, own), name='whole',...  140 us
    unnamed x14, local copies, waits for them, and re-layouts  5.48 us

profile of v5, /device:TPU:1, one launch (start us, length us, event | category | flops | bytes accessed | tf_op | source)
XLA Modules:
  0.0 148.7 jit_solution(14225423016238249547)
XLA Ops:
  0.6 0.7 pad_maximum_fusion
  1.3 0.6 reshape.28.gain_ref
  2.0 140.0 %whole.1 = (bf16[288,1024]{1,0:T(8,128)(2,1)}, bf16[128,768]{1,0:T(8,128)(2,1)}, bf16[240,768]{1,0:T(8,128)(2,1)}, bf16[288,1536]{1,0:T(8,128)(2,1)}, f32[1,768]{1,0:T(1,128)}, /*index=5*/f32[2,768]{1,0:T(2,128)}) custom-call(bf16[128,768]{1,0:T(8,128)(2,1)} %bitcast.23, bf16[240,768]{1,0:T(8,128)(2,1)} %bitcast.20, bf16[288,1536]{1,0:T(8,128)(2,1)} %bitcast.17, ...), custom_call_target="tpu_custom_call" | custom-call | tf_op jit(solution)/shard_map/whole/pallas_call | solution.py:754
  141.9 0.0 copy-start.3
  142.0 0.7 copy-done.3
  142.6 0.0 copy-start.4
  142.6 0.6 reshape.31
  143.3 0.1 copy-done.4
  143.3 0.6 reduce
  143.9 0.0 copy-start.2
  143.9 0.0 copy-start
  143.9 2.0 %copy.16 = bf16[1,1024,288]{1,2,0:T(8,128)(2,1)} copy(bf16[1,1024,288]{1,2,0:T(8,128)(2,1)} %bitcast.18) | data formatting | bytes 1179648
  145.9 0.0 copy-done.2
  145.9 0.0 copy-start.1
  145.9 0.7 copy.17
  146.6 0.4 copy-done.1
  147.0 0.7 copy.18
  147.7 0.0 copy-done
  147.7 0.9 copy.19
Async XLA Ops:
  141.9 0.7 copy-start.3
  142.6 0.7 copy-start.4
  143.9 2.0 %copy-start.2 = (bf16[128,768]{1,0:T(8,128)(2,1)S(1)}, bf16[128,768]{1,0:T(8,128)(2,1)}, u32[]{:S(2)}) copy-start(bf16[128,768]{1,0:T(8,128)(2,1)} %get-tuple-element.13) | copy-start | bytes 589828
  143.9 3.8 %copy-start = (bf16[288,1536]{1,0:T(8,128)(2,1)S(1)}, bf16[288,1536]{1,0:T(8,128)(2,1)}, u32[]{:S(2)}) copy-start(bf16[288,1536]{1,0:T(8,128)(2,1)} %get-tuple-element.17) | copy-start | bytes 2654212
  145.9 1.1 copy-start.1

commit v6 on v5

--- a/solution.py
+++ b/solution.py
@@ -630,9 +630,11 @@
                 total = term if total is None else total + term
         normed_grad[:, lanes] = total
 
-    def project(step, last=False):
+    def qkv_of(step):
         block = all_mid[pl.ds(wrap4(p.y + step) * 4, 4)].reshape(span_rows, width)
         qkv_ref[:, column_lanes(step)] = contract(wt_ref[...], block, ((1,), (1,))).astype(BF16)
+
+    def project(step, last=False):
         left = cot_ref[:, column_lanes(step)]
         for n in range(width // tile):
             span = slice(n * tile, (n + 1) * tile)
@@ -700,28 +702,32 @@
             mid.far(d)
     project(2, last=True)
     proj_sum.core()
+    qkv_of(0)
+    proj_sum.x()
     kernel_sum.x()
     gains.onward(2)
-    proj_sum.x()
+    qkv_of(1)
+    proj_sum.z()
     kernel_sum.z()
+    qkv_of(-1)
+    qkv_of(2)
+    proj_sum.zz()
     gains.onward(3)
-    proj_sum.z()
     kernel_sum.zz()
+    proj_sum.xx()
+    kernel_sum.xx()
     gain_total = gains.total(3) * scale
     gain_in_out[...] = gain_total[0:1, :]
     gain_mid_out[...] = gain_total[1:3, :]
-    proj_sum.zz()
-    kernel_sum.xx()
-    proj_sum.xx()
+    proj_sum.cc()
     kernel_sum.cc()
-    proj_sum.cc()
+    proj_sum.end()
+    proj_rows = wt_ref.shape[0]
+    for j in range(width // 128):
+        proj_ref[:, j * 128 : (j + 1) * 128] = p_out[j * proj_rows : (j + 1) * proj_rows, :]
     kernel_sum.end()
     for j in range(chans // 128):
         kernel_ref[:, j * 128 : (j + 1) * 128] = k_out[j * high : (j + 1) * high, :]
-    proj_sum.end()
-    high = wt_ref.shape[0]
-    for j in range(width // 128):
-        proj_ref[:, j * 128 : (j + 1) * 128] = p_out[j * high : (j + 1) * high, :]
     wire.drain()
 
 

time: 151 us -> 147 us (0.974)
  Pallas kernels: 140 us -> 137 us
    pallas_call x1, Pallas kernels: 140 us -> 137 us  [body(): pl.pallas_call(functools.partial(whole_kernel, scale, own), name='whole',...]
where the time goes in v6:
time: 147 us; the launch traced here: 145 us
  Pallas kernels  137 us (93%)
  local copies, waits for them, and re-layouts  6.7 us (5%)
    pallas_call x1, Pallas kernels, body(): pl.pallas_call(functools.partial(whole_kernel, scale, own), name='whole',...  137 us
    unnamed x14, local copies, waits for them, and re-layouts  5.48 us

profile of v6, /device:TPU:1, one launch (start us, length us, event | category | flops | bytes accessed | tf_op | source)
XLA Modules:
  0.0 145.2 jit_solution(3238198930537732267)
XLA Ops:
  0.6 0.7 pad_maximum_fusion
  1.3 0.6 reshape.28.gain_ref
  2.0 136.6 %whole.1 = (bf16[288,1024]{1,0:T(8,128)(2,1)}, bf16[128,768]{1,0:T(8,128)(2,1)}, bf16[240,768]{1,0:T(8,128)(2,1)}, bf16[288,1536]{1,0:T(8,128)(2,1)}, f32[1,768]{1,0:T(1,128)}, /*index=5*/f32[2,768]{1,0:T(2,128)}) custom-call(bf16[128,768]{1,0:T(8,128)(2,1)} %bitcast.23, bf16[240,768]{1,0:T(8,128)(2,1)} %bitcast.20, bf16[288,1536]{1,0:T(8,128)(2,1)} %bitcast.17, ...), custom_call_target="tpu_custom_call" | custom-call | tf_op jit(solution)/shard_map/whole/pallas_call | solution.py:760
  138.5 0.0 copy-start.3
  138.5 0.7 copy-done.3
  139.2 0.0 copy-start.4
  139.2 0.6 reshape.31
  139.8 0.1 copy-done.4
  139.9 0.6 reduce
  140.5 0.0 copy-start.2
  140.5 0.0 copy-start
  140.5 2.0 %copy.16 = bf16[1,1024,288]{1,2,0:T(8,128)(2,1)} copy(bf16[1,1024,288]{1,2,0:T(8,128)(2,1)} %bitcast.18) | data formatting | bytes 1179648
  142.5 0.0 copy-done.2
  142.5 0.0 copy-start.1
  142.5 0.7 copy.17
  143.2 0.4 copy-done.1
  143.6 0.7 copy.18
  144.3 0.0 copy-done
  144.3 0.9 copy.19
Async XLA Ops:
  138.5 0.7 copy-start.3
  139.2 0.7 copy-start.4
  140.5 2.0 %copy-start.2 = (bf16[128,768]{1,0:T(8,128)(2,1)S(1)}, bf16[128,768]{1,0:T(8,128)(2,1)}, u32[]{:S(2)}) copy-start(bf16[128,768]{1,0:T(8,128)(2,1)} %get-tuple-element.13) | copy-start | bytes 589828
  140.5 3.8 %copy-start = (bf16[288,1536]{1,0:T(8,128)(2,1)S(1)}, bf16[288,1536]{1,0:T(8,128)(2,1)}, u32[]{:S(2)}) copy-start(bf16[288,1536]{1,0:T(8,128)(2,1)} %get-tuple-element.17) | copy-start | bytes 2654212
  142.5 1.1 copy-start.1
